TPU v7x, 32 devices: a whole 2x2x4 slice. The times are simulated.
32 devices in a mesh: vis: 8 (over z, x), tile: 4 (over y, core).
Axes of the slice: x: 2, y: 2, z: 4, core: 2. Of those that a mesh axis runs over, the one named last changes fastest.
Arguments:
- vis_data: bfloat16 [32768, 128], P(('vis', 'tile')), may hold values from -0.59765625 to 0.59765625
- u_cell: int32 [16, 32768], P(None, ('vis', 'tile')), may hold values from 0 to 25
- v_cell: int32 [16, 32768], P(None, ('vis', 'tile')), may hold values from 0 to 25
- u_frac: int32 [16, 32768], P(None, ('vis', 'tile')), may hold values from 0 to 15
- v_frac: int32 [16, 32768], P(None, ('vis', 'tile')), may hold values from 0 to 15
- w_plane: int32 [16, 32768], P(None, ('vis', 'tile')), may hold values from 0 to 7
- block_route: int32 [32768, 1], P(('vis', 'tile')), may hold values from 0 to 63; in each aligned block of 1024 rows (0 to 1023, 1024 to 2047, ...) at most 32 rows name the same one
- kernel_taps: float32 [128, 7], replicated, may hold values from 0.1 to 1
- taper_gain: float32 [32, 32], replicated, may hold values from 0.2 to 1
- sub_tile: int32 [256, 1], P(('vis', 'tile')), may hold values from 0 to 7; in each aligned block of 8 rows (0 to 7, 8 to 15, ...) at most 2 rows name the same one
- sub_anchor: int32 [256, 2], P(('vis', 'tile')), may hold values from 0 to 224
Outputs:
- grid_sum: float32 [8, 256, 2048], P('tile', 'vis')
Inputs may be any that keep to these rules, and one draw needn't show every extreme that they name: `block_route`: among the rows of one device at most 32 name one uv-block, and some uv-block is named by exactly 32 of them. `sub_tile`: among the 8 uv-blocks of one device at most 2 map to one grid tile, and some grid tile gets exactly 2 of them.
All inputs are finite; a program needn't handle non-finite values.
Results may differ from a plain program's by a relative error of at most 0.008.
Values may be sent and summed in bfloat16 or wider, within the bound.
A program may use at most 128 MiB of HBM per device.

v0:
```python
import functools

import jax
import jax.numpy as jnp
from jax import lax
from jax.experimental import pallas as pl
from jax.experimental.pallas import tpu as pltpu
from jax.sharding import PartitionSpec as P

BLK_DEV = 8
SUB = 32
POLC = 8
TAPS = 7
OS = 16
TS = 256
GT = 8
SCAP = 2
LANES = 128
ROWS = 8
GROUP = 4
FAR = 1 << 20
MESH = pl.DeviceIdType.MESH
NT = (((1,), (1,)), ((), ()))


def dispatch_kernel(
    slot_cap, vis, u_cell, v_cell, u_frac, v_frac, w_plane, route, taps, gain, out, table, taper, feat, dest
):
    rows = vis.shape[0]
    columns = vis.shape[1]
    channels = u_cell.shape[0]
    owners, _, chunk = out.shape
    groups = owners * BLK_DEV
    feat[pl.ds(0, columns), :] = vis[...].astype(jnp.float32).T.astype(jnp.bfloat16)
    plane = w_plane[...] * OS
    codes = (u_cell[...], v_cell[...], plane + u_frac[...], plane + v_frac[...])
    for place, code in enumerate(codes):
        feat[pl.ds(columns + place * channels, channels), :] = code.astype(jnp.float32).astype(
            jnp.bfloat16
        )
    names = route[...]
    mine = lax.broadcasted_iota(jnp.int32, (groups, rows), 0) == names
    onehot = jnp.where(mine, 1.0, 0.0)
    earlier = lax.broadcasted_iota(jnp.int32, (rows, rows), 0) < lax.broadcasted_iota(
        jnp.int32, (rows, rows), 1
    )
    before = jnp.dot(
        onehot.astype(jnp.bfloat16),
        jnp.where(earlier, 1.0, 0.0).astype(jnp.bfloat16),
        preferred_element_type=jnp.float32,
    )
    rank = jnp.sum(onehot * before, axis=0, keepdims=True).astype(jnp.int32)
    dest[...] = names * slot_cap + rank

    turn = lax.broadcasted_iota(jnp.int32, (ROWS, TAPS), 0) == lax.broadcasted_iota(
        jnp.int32, (ROWS, TAPS), 1
    )
    table[...] = lax.dot_general(
        jnp.where(turn, 1.0, 0.0).astype(jnp.bfloat16),
        taps[...].astype(jnp.bfloat16),
        NT,
        preferred_element_type=jnp.float32,
    )
    cells = lax.broadcasted_iota(jnp.int32, (SUB, SUB * POLC), 0)
    repeat = cells == lax.broadcasted_iota(jnp.int32, (SUB, SUB * POLC), 1) // POLC
    taper[...] = jnp.dot(
        gain[...],
        jnp.where(repeat, 1.0, 0.0),
        precision=lax.Precision.HIGHEST,
        preferred_element_type=jnp.float32,
    )

    def send(owner, _):
        slots = lax.broadcasted_iota(jnp.int32, (chunk, rows), 0) + owner * chunk
        pick = jnp.where(slots == dest[...], 1.0, 0.0).astype(jnp.bfloat16)
        out[owner] = lax.dot_general(
            feat[...], pick, NT, preferred_element_type=jnp.float32
        ).astype(jnp.bfloat16)
        return 0

    lax.fori_loop(0, owners, send, 0)


def spread(cell, taps):
    rows = lax.broadcasted_iota(jnp.int32, taps.shape, 0) - cell
    parts = []
    for start in range(0, SUB, ROWS):
        delta = rows + start
        weight = jnp.take_along_axis(taps, delta & (ROWS - 1), axis=0)
        parts.append(jnp.where((delta >= 0) & (delta < ROWS), weight, 0.0))
    return jnp.concatenate(parts, axis=0)


def grid_chunk(slot_cap, chunk, channels, lane, feat, table, total, left, right):
    covered = min(BLK_DEV, LANES // slot_cap)
    first = lane % chunk // slot_cap
    columns = channels * POLC
    lanes = lax.broadcasted_iota(jnp.int32, (SUB, LANES), 1)
    block = (lane + lanes) % chunk // slot_cap - first
    samples = feat[:columns, :].astype(jnp.float32)
    codes = feat[columns:, :].astype(jnp.float32).astype(jnp.int32)
    lookup = table[...]
    part = jnp.zeros((covered * SUB, SUB * POLC), jnp.float32)
    for h in range(channels):
        sample = samples[h * POLC : (h + 1) * POLC, :]
        cell_u = codes[h : h + 1, :]
        cell_v = codes[channels + h : channels + h + 1, :]
        row_u = codes[2 * channels + h : 2 * channels + h + 1, :]
        row_v = codes[3 * channels + h : 3 * channels + h + 1, :]
        taps_u = jnp.take_along_axis(lookup, jnp.broadcast_to(row_u, (8, LANES)), axis=1)
        taps_v = jnp.take_along_axis(lookup, jnp.broadcast_to(row_v, (8, LANES)), axis=1)
        weight_u = spread(cell_u, taps_u)
        weight_v = spread(cell_v, taps_v)
        here = pl.ds(h * LANES, LANES)
        weighted = weight_u[:, None, :] * sample[None, :, :]
        right[:, here] = weighted.reshape(SUB * POLC, LANES).astype(jnp.bfloat16)
        for b in range(covered):
            left[pl.ds(b * SUB, SUB), here] = jnp.where(block == b, weight_v, 0.0).astype(
                jnp.bfloat16
            )
        if (h + 1) % GROUP == 0:
            group = pl.ds((h + 1 - GROUP) * LANES, GROUP * LANES)
            part = part + lax.dot_general(
                left[:, group], right[:, group], NT, preferred_element_type=jnp.float32
            )
    place = pl.ds(pl.multiple_of(first * SUB, SUB), covered * SUB)
    total[place, :] = total[place, :] + part


def grid_kernel(slot_cap, chunk, channels, feat, table, taper, out, total, left, right):
    step = pl.program_id(0)

    @pl.when(step == 0)
    def _():
        total[...] = jnp.zeros_like(total)

    grid_chunk(
        slot_cap, chunk, channels, step * LANES, feat[0], table, total, left, right
    )

    @pl.when(step == pl.num_programs(0) - 1)
    def _():
        for b in range(BLK_DEV):
            out[b] = (total[pl.ds(b * SUB, SUB), :] * taper[...]).astype(jnp.bfloat16)


def move_grid_kernel(
    slot_cap, channels, send, table, taper, out, moved, total, left, right, own_sem, to_sem, at_sem
):
    count, features, chunk = send.shape
    v, t = lax.axis_index("vis"), lax.axis_index("tile")
    barrier = pltpu.get_barrier_semaphore()
    for k in range(1, count):
        pl.semaphore_signal(barrier, inc=1, device_id=((v + k) % count, t), device_id_type=MESH)
    pl.semaphore_wait(barrier, count - 1)

    def copy(k):
        return pltpu.make_async_remote_copy(
            src_ref=send.at[(v + k) % count],
            dst_ref=moved.at[v],
            send_sem=to_sem.at[k],
            recv_sem=at_sem.at[k],
            device_id=((v + k) % count, t),
            device_id_type=MESH,
        )

    own = pltpu.make_async_copy(send.at[v], moved.at[v], own_sem.at[0])
    own.start()
    for k in range(1, count):
        copy(k).start()
    total[...] = jnp.zeros_like(total)
    own.wait()

    def source(k, _):
        @pl.when(k > 0)
        def _():
            copy(k).wait_recv()

        origin = (v + count - k) % count

        def part(piece, _):
            lane = pl.multiple_of(piece * LANES, LANES)
            grid_chunk(
                slot_cap,
                chunk,
                channels,
                lane,
                moved[origin, :, pl.ds(lane, LANES)],
                table,
                total,
                left,
                right,
            )
            return 0

        lax.fori_loop(0, chunk // LANES, part, 0)
        return 0

    lax.fori_loop(0, count, source, 0)
    for b in range(BLK_DEV):
        out[b] = (total[pl.ds(b * SUB, SUB), :] * taper[...]).astype(jnp.bfloat16)
    for k in range(1, count):
        copy(k).wait_send()


def slot_kernel(tiles, anchors, subs, out, meta):
    slots = out.shape[0]
    out[...] = jnp.zeros_like(out)
    lanes = lax.broadcasted_iota(jnp.int32, meta.shape, 1)
    places = jnp.full(meta.shape, -FAR, jnp.int32)
    for b in range(BLK_DEV):
        slot = tiles[b, 0] * SCAP
        for before in range(b):
            slot = slot + jnp.where(tiles[before, 0] == tiles[b, 0], 1, 0)
        out[slot] = subs[b]
        places = jnp.where(lanes == slot, anchors[b, 0], places)
        places = jnp.where(lanes == slots + slot, anchors[b, 1], places)
    meta[...] = places


def gather_kernel(subs, meta, out, meta_out, own_sem, near_send, near_recv, far_send, far_recv):
    count = out.shape[0]
    width = out.shape[1]
    v, t = lax.axis_index("vis"), lax.axis_index("tile")
    half = count // 2
    spot = v // 2 * (1 - v % 2) + (count - 1 - v // 2) * (v % 2)

    def member(position):
        position = (position + 2 * count) % count
        back = position // half
        return (1 - back) * 2 * position + back * (2 * (count - 1 - position) + 1)

    barrier = pltpu.get_barrier_semaphore()
    for side in (1, -1):
        pl.semaphore_signal(
            barrier, inc=1, device_id=(member(spot + side), t), device_id_type=MESH
        )
    for k in range(1, width):
        pl.semaphore_signal(barrier, inc=1, device_id=(v, (t + k) % width), device_id_type=MESH)
    pl.semaphore_wait(barrier, 1 + width)

    def near(k):
        chunk = pl.ds((t + k) % width, 1)
        pairs = ((subs.at[chunk], out.at[v, pl.ds(t, 1)]), (meta, meta_out.at[v, t]))
        return [
            pltpu.make_async_remote_copy(
                src_ref=src,
                dst_ref=dst,
                send_sem=near_send.at[2 * k + i],
                recv_sem=near_recv.at[2 * k + i],
                device_id=(v, (t + k) % width),
                device_id_type=MESH,
            )
            for i, (src, dst) in enumerate(pairs)
        ]

    def own():
        pairs = ((subs.at[pl.ds(t, 1)], out.at[v, pl.ds(t, 1)]), (meta, meta_out.at[v, t]))
        return [
            pltpu.make_async_copy(src, dst, own_sem.at[i]) for i, (src, dst) in enumerate(pairs)
        ]

    def far(k, step):
        source = (t + width - k) % width
        cut = out.shape[2] // 2
        copies = []
        for i in range(3):
            side = 1 - 2 * (i % 2)
            origin = member(spot - side * step)
            if i < 2:
                ref = out.at[origin, source, pl.ds(i * cut, cut)]
            else:
                ref = meta_out.at[origin, source]
            copies.append(
                pltpu.make_async_remote_copy(
                    src_ref=ref,
                    dst_ref=ref,
                    send_sem=far_send.at[(step * width + k) * 3 + i],
                    recv_sem=far_recv.at[(step * width + k) * 3 + i],
                    device_id=(member(spot + side), t),
                    device_id_type=MESH,
                )
            )
        return copies

    for copy in own():
        copy.start()
    for k in range(1, width):
        for copy in near(k):
            copy.start()
    for copy in own():
        copy.wait()
    for k in range(width):
        if k:
            for copy in near(k):
                copy.wait_recv()
        for copy in far(k, 0):
            copy.start()

    def forward(step, _):
        for k in range(width):
            for landed, copy in zip(far(k, step - 1), far(k, step)):
                landed.wait_recv()
                copy.start()
        return 0

    lax.fori_loop(1, count - 1, forward, 0)
    for k in range(width):
        for copy in far(k, count - 2):
            copy.wait_recv()
    for k in range(1, width):
        for copy in near(k):
            copy.wait_send()

    def sent(step, _):
        for k in range(width):
            for copy in far(k, step):
                copy.wait_send()
        return 0

    lax.fori_loop(0, count - 1, sent, 0)


def place_kernel(tile_slots, meta, subs, out, canvas):
    v, t = lax.axis_index("vis"), lax.axis_index("tile")
    step = pl.program_id(0)
    slots = subs.shape[1]
    height = out.shape[1]
    width = out.shape[2]
    span = SUB * POLC

    @pl.when(step == 0)
    def _():
        canvas[...] = jnp.zeros_like(canvas)

    def add_source(near, _):
        source = step * (slots // tile_slots) + near
        for slot in range(tile_slots):
            lane = t * tile_slots + slot
            low = meta[source, lane] - v * height + SUB
            column = meta[source, slots + lane] * POLC

            @pl.when((low > 0) & (low < height + SUB))
            def _():
                sub = subs[0, near * tile_slots + slot].astype(jnp.float32)
                sub = jnp.concatenate([sub, jnp.zeros((SUB, LANES), jnp.float32)], axis=1)
                sub = pltpu.roll(sub, column % LANES, 1)
                sub = jnp.concatenate([sub, jnp.zeros((ROWS, span + LANES), jnp.float32)], axis=0)
                sub = pltpu.roll(sub, low % ROWS, 0)
                top = pl.multiple_of(low // ROWS * ROWS, ROWS)
                base = pl.multiple_of(column // LANES * LANES, LANES)
                here = (slot // SCAP, pl.ds(top, SUB + ROWS), pl.ds(base, span + LANES))
                canvas[here] = canvas[here] + sub

        return 0

    lax.fori_loop(0, slots // tile_slots, add_source, 0)

    @pl.when(step == pl.num_programs(0) - 1)
    def _():
        out[...] = canvas[:, pl.ds(SUB, height), pl.ds(0, width)]


def on_device(
    vis_data,
    u_cell,
    v_cell,
    u_frac,
    v_frac,
    w_plane,
    block_route,
    kernel_taps,
    taper_gain,
    sub_tile,
    sub_anchor,
):
    vis_count = lax.axis_size("vis")
    tile_width = lax.axis_size("tile")
    gt_dev = GT // tile_width
    rows, columns = vis_data.shape
    channels = u_cell.shape[0]
    slot_cap = max(2, 2 * rows // (BLK_DEV * vis_count))
    chunk = BLK_DEV * slot_cap
    features = columns + 4 * channels
    per_owner = gt_dev * SCAP
    slots = tile_width * per_owner
    height = TS // vis_count
    width = TS * POLC

    send, table, taper = pl.pallas_call(
        functools.partial(dispatch_kernel, slot_cap),
        out_shape=[
            jax.ShapeDtypeStruct((vis_count, features, chunk), jnp.bfloat16),
            jax.ShapeDtypeStruct((ROWS, LANES), jnp.float32),
            jax.ShapeDtypeStruct((SUB, SUB * POLC), jnp.float32),
        ],
        scratch_shapes=[
            pltpu.VMEM((features, rows), jnp.bfloat16),
            pltpu.VMEM((1, rows), jnp.int32),
        ],
        name="dispatch",
    )(
        vis_data,
        u_cell,
        v_cell,
        u_frac,
        v_frac,
        w_plane,
        block_route.reshape(1, rows),
        kernel_taps,
        taper_gain,
    )
    covered = min(BLK_DEV, LANES // slot_cap)
    vmem = pl.BlockSpec(memory_space=pltpu.VMEM)
    work = [
        pltpu.VMEM((BLK_DEV * SUB, SUB * POLC), jnp.float32),
        pltpu.VMEM((covered * SUB, channels * LANES), jnp.bfloat16),
        pltpu.VMEM((SUB * POLC, channels * LANES), jnp.bfloat16),
    ]
    gridded = jax.ShapeDtypeStruct((BLK_DEV, SUB, SUB * POLC), jnp.bfloat16)
    if chunk % LANES == 0:
        subs = pl.pallas_call(
            functools.partial(move_grid_kernel, slot_cap, channels),
            in_specs=[vmem, vmem, vmem],
            out_specs=vmem,
            out_shape=gridded,
            scratch_shapes=[pltpu.VMEM(send.shape, jnp.bfloat16)]
            + work
            + [
                pltpu.SemaphoreType.DMA((1,)),
                pltpu.SemaphoreType.DMA((vis_count,)),
                pltpu.SemaphoreType.DMA((vis_count,)),
            ],
            compiler_params=pltpu.CompilerParams(collective_id=1, has_side_effects=True),
            name="move_grid",
        )(send, table, taper)
    else:
        moved = lax.all_to_all(send, "vis", split_axis=0, concat_axis=0, tiled=True)
        moved = jnp.transpose(moved, (1, 0, 2)).reshape(1, features, vis_count * chunk)
        subs = pl.pallas_call(
            functools.partial(grid_kernel, slot_cap, chunk, channels),
            grid=(moved.shape[2] // LANES,),
            in_specs=[
                pl.BlockSpec((1, features, LANES), lambda s: (0, 0, s)),
                pl.BlockSpec(table.shape, lambda s: (0, 0)),
                pl.BlockSpec(taper.shape, lambda s: (0, 0)),
            ],
            out_specs=pl.BlockSpec(gridded.shape, lambda s: (0, 0, 0)),
            out_shape=gridded,
            scratch_shapes=work,
            name="grid",
        )(moved, table, taper)
    scalars = pl.BlockSpec(memory_space=pltpu.SMEM)
    subs, meta = pl.pallas_call(
        slot_kernel,
        in_specs=[scalars, scalars, vmem],
        out_specs=[vmem, vmem],
        out_shape=[
            jax.ShapeDtypeStruct((slots, SUB, SUB * POLC), jnp.bfloat16),
            jax.ShapeDtypeStruct((1, LANES), jnp.int32),
        ],
        name="slot",
    )(sub_tile, sub_anchor, subs)
    hops = (vis_count - 1) * tile_width * 3
    subs, meta = pl.pallas_call(
        gather_kernel,
        in_specs=[vmem, vmem],
        out_specs=[vmem, vmem],
        out_shape=[
            jax.ShapeDtypeStruct(
                (vis_count, tile_width, per_owner, SUB, SUB * POLC), jnp.bfloat16
            ),
            jax.ShapeDtypeStruct((vis_count, tile_width, 1, LANES), jnp.int32),
        ],
        scratch_shapes=[
            pltpu.SemaphoreType.DMA((2,)),
            pltpu.SemaphoreType.DMA((2 * tile_width,)),
            pltpu.SemaphoreType.DMA((2 * tile_width,)),
            pltpu.SemaphoreType.DMA((hops,)),
            pltpu.SemaphoreType.DMA((hops,)),
        ],
        compiler_params=pltpu.CompilerParams(collective_id=0, has_side_effects=True),
        name="gather",
    )(subs.reshape(tile_width, per_owner, SUB, SUB * POLC), meta)
    subs = subs.reshape(vis_count, slots, SUB, SUB * POLC)
    meta = meta.reshape(vis_count * tile_width, LANES)
    return pl.pallas_call(
        functools.partial(place_kernel, per_owner),
        grid_spec=pltpu.PrefetchScalarGridSpec(
            num_scalar_prefetch=1,
            grid=(vis_count,),
            in_specs=[pl.BlockSpec((1, slots, SUB, SUB * POLC), lambda s, *_: (s, 0, 0, 0))],
            out_specs=pl.BlockSpec((gt_dev, height, width), lambda s, *_: (0, 0, 0)),
            scratch_shapes=[
                pltpu.VMEM((gt_dev, -(-height // ROWS) * ROWS + 2 * SUB + ROWS, width + LANES), jnp.float32),
            ],
        ),
        out_shape=jax.ShapeDtypeStruct((gt_dev, height, width), jnp.float32),
        name="place",
    )(meta, subs)


def solution(mesh):
    placed = (
        P(("vis", "tile"), None),
        P(None, ("vis", "tile")),
        P(None, ("vis", "tile")),
        P(None, ("vis", "tile")),
        P(None, ("vis", "tile")),
        P(None, ("vis", "tile")),
        P(("vis", "tile"), None),
        P(),
        P(),
        P(("vis", "tile"), None),
        P(("vis", "tile"), None),
    )
    return jax.shard_map(
        on_device, mesh=mesh, in_specs=placed, out_specs=P("tile", "vis", None), check_vma=False
    )
```

profile of v0, /device:TPU:0, one launch (start us, length us, event | category | flops | bytes accessed | tf_op | source)
XLA Modules:
  0.0 86.1 jit_solution(11509528332498843123)
XLA Ops:
  0.0 1.3 %copy.13.tiles = s32[8,1]{1,0:T(8,128)} copy(s32[8,1]{0,1:T(1,128)} %param.20) | data formatting | bytes 64 | tf_op args[9]
  1.3 1.3 %copy.14.anchors = s32[8,2]{1,0:T(8,128)} copy(s32[8,2]{0,1:T(2,128)} %param.21) | data formatting | bytes 128 | tf_op args[10]
  2.7 1.4 %copy.12.taps = f32[128,7]{1,0:T(8,128)} copy(f32[128,7]{0,1:T(8,128)} %param.18) | data formatting | bytes 7168 | tf_op args[7]
  4.1 5.4 %dispatch.1 = (bf16[8,192,256]{2,1,0:T(8,128)(2,1)}, f32[8,128]{1,0:T(8,128)}, f32[32,256]{1,0:T(8,128)}) custom-call(bf16[1024,128]{1,0:T(8,128)(2,1)} %vis.1, s32[16,1024]{1,0:T(8,128)} %u_cell.1, s32[16,1024]{1,0:T(8,128)} %v_cell.1, s32[16,1024]{1,0:T(8,128)} %u_frac.1, s32[16,1024]{1,0:T(8,128)} %v_frac.1, s32[16,1024]{1,0:T(8,128)} %w_plane.1, ...), custom_call_target="tpu_custom_call" | custom-call | tf_op jit(solution)/shard_map/dispatch/pallas_call | solution.py:390
  9.5 30.8 %move_grid.1.subs = bf16[8,32,256]{2,1,0:T(8,128)(2,1)} custom-call(bf16[8,192,256]{2,1,0:T(8,128)(2,1)} %get-tuple-element.12.send, f32[8,128]{1,0:T(8,128)} %get-tuple-element.13.table, f32[32,256]{1,0:T(8,128)} %get-tuple-element.14.taper), custom_call_target="tpu_custom_call" | custom-call | tf_op jit(solution)/shard_map/move_grid/pallas_call | solution.py:422
  40.3 1.7 %slot.1 = (bf16[16,32,256]{2,1,0:T(8,128)(2,1)}, s32[1,128]{1,0:T(1,128)}) custom-call(s32[8,1]{1,0:T(8,128)} %copy.13.tiles, s32[8,2]{1,0:T(8,128)} %copy.14.anchors, bf16[8,32,256]{2,1,0:T(8,128)(2,1)} %move_grid.1.subs), custom_call_target="tpu_custom_call" | custom-call | tf_op jit(solution)/shard_map/slot/pallas_call | solution.py:454
  41.9 37.1 %gather.1 = (bf16[8,4,4,32,256]{4,3,2,1,0:T(8,128)(2,1)}, s32[8,4,1,128]{3,2,1,0:T(1,128)}) custom-call(bf16[4,4,32,256]{3,2,1,0:T(8,128)(2,1)} %bitcast.5, s32[1,128]{1,0:T(1,128)} %get-tuple-element.16.meta), custom_call_target="tpu_custom_call" | custom-call | tf_op jit(solution)/shard_map/gather/pallas_call | solution.py:465
  79.1 7.0 %place.1 = f32[2,32,2048]{2,1,0:T(8,128)} custom-call(s32[32,128]{1,0:T(8,128)} %bitcast.6, bf16[8,16,32,256]{3,2,1,0:T(8,128)(2,1)} %bitcast.4), custom_call_target="tpu_custom_call" | custom-call | tf_op jit(solution)/shard_map/place/pallas_call | solution.py:487
where the time goes:
time: 86.5 us; the launch traced here: 86.1 us
  Pallas kernels  82 us (95%)
  local copies, waits for them, and re-layouts  4.08 us (5%)
    pallas_call x1, Pallas kernels, on_device(): pl.pallas_call(gather_kernel, in_specs=[vmem, vmem], out_specs=[vmem, vme...  37.1 us
    pallas_call x1, Pallas kernels, on_device(): pl.pallas_call(functools.partial(move_grid_kernel, slot_cap, channels), i...  30.8 us
    pallas_call x1, Pallas kernels, on_device(): pl.pallas_call(functools.partial(place_kernel, per_owner), grid_spec=pltp...  6.98 us
    pallas_call x1, Pallas kernels, on_device(): pl.pallas_call(functools.partial(dispatch_kernel, slot_cap), out_shape=[j...  5.4 us
    unnamed x3, local copies, waits for them, and re-layouts  4.08 us

commit v1 on v0

--- a/solution.py
+++ b/solution.py
@@ -24,7 +24,7 @@
 
 
 def dispatch_kernel(
-    slot_cap, vis, u_cell, v_cell, u_frac, v_frac, w_plane, route, taps, gain, out, table, taper, feat, dest
+    slot_cap, regroup, vis, u_cell, v_cell, u_frac, v_frac, w_plane, route, taps, gain, out, table, taper, feat, dest
 ):
     rows = vis.shape[0]
     columns = vis.shape[1]
@@ -34,10 +34,18 @@
     feat[pl.ds(0, columns), :] = vis[...].astype(jnp.float32).T.astype(jnp.bfloat16)
     plane = w_plane[...] * OS
     codes = (u_cell[...], v_cell[...], plane + u_frac[...], plane + v_frac[...])
-    for place, code in enumerate(codes):
-        feat[pl.ds(columns + place * channels, channels), :] = code.astype(jnp.float32).astype(
-            jnp.bfloat16
-        )
+    codes = jnp.concatenate(codes, axis=0).astype(jnp.float32).astype(jnp.bfloat16)
+    if regroup:
+        count = 4 * channels
+        width = channels // GROUP
+        to = lax.broadcasted_iota(jnp.int32, (count, count), 0)
+        quarter, rest = to // (4 * width), to % (4 * width)
+        source = rest // width * channels + quarter * width + rest % width
+        turn = source == lax.broadcasted_iota(jnp.int32, (count, count), 1)
+        codes = jnp.dot(
+            jnp.where(turn, 1.0, 0.0).astype(jnp.bfloat16), codes, preferred_element_type=jnp.float32
+        ).astype(jnp.bfloat16)
+    feat[pl.ds(columns, 4 * channels), :] = codes
     names = route[...]
     mine = lax.broadcasted_iota(jnp.int32, (groups, rows), 0) == names
     onehot = jnp.where(mine, 1.0, 0.0)
@@ -52,15 +60,8 @@
     rank = jnp.sum(onehot * before, axis=0, keepdims=True).astype(jnp.int32)
     dest[...] = names * slot_cap + rank
 
-    turn = lax.broadcasted_iota(jnp.int32, (ROWS, TAPS), 0) == lax.broadcasted_iota(
-        jnp.int32, (ROWS, TAPS), 1
-    )
-    table[...] = lax.dot_general(
-        jnp.where(turn, 1.0, 0.0).astype(jnp.bfloat16),
-        taps[...].astype(jnp.bfloat16),
-        NT,
-        preferred_element_type=jnp.float32,
-    )
+    table[...] = jnp.zeros_like(table)
+    table[pl.ds(0, TAPS), :] = taps[...].astype(jnp.bfloat16).astype(jnp.float32)
     cells = lax.broadcasted_iota(jnp.int32, (SUB, SUB * POLC), 0)
     repeat = cells == lax.broadcasted_iota(jnp.int32, (SUB, SUB * POLC), 1) // POLC
     taper[...] = jnp.dot(
@@ -144,8 +145,65 @@
             out[b] = (total[pl.ds(b * SUB, SUB), :] * taper[...]).astype(jnp.bfloat16)
 
 
+def swap(first, second, width):
+    low = lax.broadcasted_iota(jnp.int32, first.shape, 1) // width % 2 == 0
+    return (
+        jnp.where(low, first, pltpu.roll(second, width, 1)),
+        jnp.where(low, pltpu.roll(first, LANES - width, 1), second),
+    )
+
+
+def regroup_lanes(parts):
+    quarter = LANES // GROUP
+    first, second = swap(parts[0], parts[1], quarter)
+    third, fourth = swap(parts[2], parts[3], quarter)
+    first, third = swap(first, third, 2 * quarter)
+    second, fourth = swap(second, fourth, 2 * quarter)
+    return first, second, third, fourth
+
+
+def weights(cell, taps):
+    delta = lax.broadcasted_iota(jnp.int32, taps.shape, 0) - cell
+    turned = jnp.take_along_axis(taps, delta & (ROWS - 1), axis=0)
+    octave = delta >> 3
+    return [jnp.where(octave == -g, turned, 0.0) for g in range(SUB // ROWS)]
+
+
+def grid_part(channels, features, table, left, right, spare):
+    width = channels // GROUP
+    columns = channels * POLC
+    span = width * POLC
+    samples = regroup_lanes([features[q * span : (q + 1) * span] for q in range(GROUP)])
+    start = [columns + q * 4 * width for q in range(GROUP)]
+    codes = regroup_lanes([features[at : at + 4 * width] for at in start])
+    lookup = table[...]
+    parts = []
+    for b in range(GROUP):
+        code = codes[b].astype(jnp.int32)
+        for g in range(width):
+            sample = samples[b][g * POLC : (g + 1) * POLC, :]
+            cell_u, cell_v, row_u, row_v = [
+                code[kind * width + g : kind * width + g + 1, :] for kind in range(4)
+            ]
+            taps_u = jnp.take_along_axis(lookup, jnp.broadcast_to(row_u, (8, LANES)), axis=1)
+            taps_v = jnp.take_along_axis(lookup, jnp.broadcast_to(row_v, (8, LANES)), axis=1)
+            here = pl.ds(g * LANES, LANES)
+            for place, weight in enumerate(weights(cell_u, taps_u)):
+                spare[g, pl.ds(place * ROWS, ROWS), :] = weight
+            for u in range(0, SUB, 2):
+                pair = [spare[g, pl.ds(u + i, POLC, stride=0), :] * sample for i in range(2)]
+                right[b, pl.ds(u * POLC, 2 * POLC), here] = jnp.concatenate(pair, axis=0).astype(
+                    jnp.bfloat16
+                )
+            left[b, :, here] = jnp.concatenate(weights(cell_v, taps_v), axis=0).astype(jnp.bfloat16)
+        parts.append(
+            lax.dot_general(left[b], right[b], NT, preferred_element_type=jnp.float32)
+        )
+    return parts
+
+
 def move_grid_kernel(
-    slot_cap, channels, send, table, taper, out, moved, total, left, right, own_sem, to_sem, at_sem
+    channels, send, table, taper, out, moved, total, left, right, spare, own_sem, to_sem, at_sem
 ):
     count, features, chunk = send.shape
     v, t = lax.axis_index("vis"), lax.axis_index("tile")
@@ -178,22 +236,12 @@
 
         origin = (v + count - k) % count
 
-        def part(piece, _):
-            lane = pl.multiple_of(piece * LANES, LANES)
-            grid_chunk(
-                slot_cap,
-                chunk,
-                channels,
-                lane,
-                moved[origin, :, pl.ds(lane, LANES)],
-                table,
-                total,
-                left,
-                right,
-            )
-            return 0
-
-        lax.fori_loop(0, chunk // LANES, part, 0)
+        for piece in range(chunk // LANES):
+            features = moved[origin, :, pl.ds(piece * LANES, LANES)].astype(jnp.float32)
+            parts = grid_part(channels, features, table, left, right, spare)
+            for b, part in enumerate(parts):
+                here = pl.ds((piece * GROUP + b) * SUB, SUB)
+                total[here, :] = total[here, :] + part
         return 0
 
     lax.fori_loop(0, count, source, 0)
@@ -209,12 +257,12 @@
     lanes = lax.broadcasted_iota(jnp.int32, meta.shape, 1)
     places = jnp.full(meta.shape, -FAR, jnp.int32)
     for b in range(BLK_DEV):
-        slot = tiles[b, 0] * SCAP
+        slot = tiles[0, b] * SCAP
         for before in range(b):
-            slot = slot + jnp.where(tiles[before, 0] == tiles[b, 0], 1, 0)
+            slot = slot + jnp.where(tiles[0, before] == tiles[0, b], 1, 0)
         out[slot] = subs[b]
-        places = jnp.where(lanes == slot, anchors[b, 0], places)
-        places = jnp.where(lanes == slots + slot, anchors[b, 1], places)
+        places = jnp.where(lanes == slot, anchors[0, b], places)
+        places = jnp.where(lanes == slots + slot, anchors[1, b], places)
     meta[...] = places
 
 
@@ -381,6 +429,7 @@
     channels = u_cell.shape[0]
     slot_cap = max(2, 2 * rows // (BLK_DEV * vis_count))
     chunk = BLK_DEV * slot_cap
+    grouped = slot_cap * GROUP == LANES and channels % GROUP == 0
     features = columns + 4 * channels
     per_owner = gt_dev * SCAP
     slots = tile_width * per_owner
@@ -388,7 +437,7 @@
     width = TS * POLC
 
     send, table, taper = pl.pallas_call(
-        functools.partial(dispatch_kernel, slot_cap),
+        functools.partial(dispatch_kernel, slot_cap, grouped),
         out_shape=[
             jax.ShapeDtypeStruct((vis_count, features, chunk), jnp.bfloat16),
             jax.ShapeDtypeStruct((ROWS, LANES), jnp.float32),
@@ -407,7 +456,7 @@
         v_frac,
         w_plane,
         block_route.reshape(1, rows),
-        kernel_taps,
+        kernel_taps.T,
         taper_gain,
     )
     covered = min(BLK_DEV, LANES // slot_cap)
@@ -418,15 +467,18 @@
         pltpu.VMEM((SUB * POLC, channels * LANES), jnp.bfloat16),
     ]
     gridded = jax.ShapeDtypeStruct((BLK_DEV, SUB, SUB * POLC), jnp.bfloat16)
-    if chunk % LANES == 0:
+    if grouped:
         subs = pl.pallas_call(
-            functools.partial(move_grid_kernel, slot_cap, channels),
+            functools.partial(move_grid_kernel, channels),
             in_specs=[vmem, vmem, vmem],
             out_specs=vmem,
             out_shape=gridded,
             scratch_shapes=[pltpu.VMEM(send.shape, jnp.bfloat16)]
-            + work
             + [
+                work[0],
+                pltpu.VMEM((GROUP, SUB, channels // GROUP * LANES), jnp.bfloat16),
+                pltpu.VMEM((GROUP, SUB * POLC, channels // GROUP * LANES), jnp.bfloat16),
+                pltpu.VMEM((channels // GROUP, SUB, LANES), jnp.float32),
                 pltpu.SemaphoreType.DMA((1,)),
                 pltpu.SemaphoreType.DMA((vis_count,)),
                 pltpu.SemaphoreType.DMA((vis_count,)),
@@ -460,7 +512,7 @@
             jax.ShapeDtypeStruct((1, LANES), jnp.int32),
         ],
         name="slot",
-    )(sub_tile, sub_anchor, subs)
+    )(sub_tile.reshape(1, BLK_DEV), sub_anchor.T, subs)
     hops = (vis_count - 1) * tile_width * 3
     subs, meta = pl.pallas_call(
         gather_kernel,

time: 86.5 us -> 77.3 us (0.89)
  Pallas kernels: 82 us -> 76.8 us
  local copies, waits for them, and re-layouts: 4.08 us -> 0 us
    pallas_call x2, Pallas kernels: 36.2 us -> 31 us  [the longest x1 25.6 us: on_device(): pl.pallas_call(functools.partial(move_grid_kernel, channels), in_specs=[v...]
    unnamed x3 -> x0, local copies, waits for them, and re-layouts: 4.08 us -> none
where the time goes in v1:
time: 77.3 us; the launch traced here: 76.8 us
  Pallas kernels  76.8 us (99%)
    pallas_call x1, Pallas kernels, on_device(): pl.pallas_call(gather_kernel, in_specs=[vmem, vmem], out_specs=[vmem, vme...  37.1 us
    pallas_call x1, Pallas kernels, on_device(): pl.pallas_call(functools.partial(move_grid_kernel, channels), in_specs=[v...  25.6 us
    pallas_call x1, Pallas kernels, on_device(): pl.pallas_call(functools.partial(place_kernel, per_owner), grid_spec=pltp...  7.02 us
    pallas_call x1, Pallas kernels, on_device(): pl.pallas_call(functools.partial(dispatch_kernel, slot_cap, grouped), out...  5.41 us
    pallas_call x1, Pallas kernels, on_device(): pl.pallas_call(slot_kernel, in_specs=[scalars, scalars, vmem], out_specs=...  1.67 us

profile of v1, /device:TPU:0, one launch (start us, length us, event | category | flops | bytes accessed | tf_op | source)
XLA Modules:
  0.0 76.8 jit_solution(5924862041356965986)
XLA Ops:
  0.0 5.4 %dispatch.1 = (bf16[8,192,256]{2,1,0:T(8,128)(2,1)}, f32[8,128]{1,0:T(8,128)}, f32[32,256]{1,0:T(8,128)}) custom-call(bf16[1024,128]{1,0:T(8,128)(2,1)} %vis.1, s32[16,1024]{1,0:T(8,128)} %u_cell.1, s32[16,1024]{1,0:T(8,128)} %v_cell.1, s32[16,1024]{1,0:T(8,128)} %u_frac.1, s32[16,1024]{1,0:T(8,128)} %v_frac.1, s32[16,1024]{1,0:T(8,128)} %w_plane.1, ...), custom_call_target="tpu_custom_call" | custom-call | tf_op jit(solution)/shard_map/dispatch/pallas_call | solution.py:439
  5.4 25.6 %move_grid.1.subs = bf16[8,32,256]{2,1,0:T(8,128)(2,1)} custom-call(bf16[8,192,256]{2,1,0:T(8,128)(2,1)} %get-tuple-element.12.send, f32[8,128]{1,0:T(8,128)} %get-tuple-element.13.table, f32[32,256]{1,0:T(8,128)} %get-tuple-element.14.taper), custom_call_target="tpu_custom_call" | custom-call | tf_op jit(solution)/shard_map/move_grid/pallas_call | solution.py:471
  31.0 1.7 %slot.1 = (bf16[16,32,256]{2,1,0:T(8,128)(2,1)}, s32[1,128]{1,0:T(1,128)}) custom-call(s32[1,8]{1,0:T(1,128)} %bitcast.13, s32[2,8]{1,0:T(2,128)} %bitcast.12, bf16[8,32,256]{2,1,0:T(8,128)(2,1)} %move_grid.1.subs), custom_call_target="tpu_custom_call" | custom-call | tf_op jit(solution)/shard_map/slot/pallas_call | solution.py:506
  32.7 37.1 %gather.1 = (bf16[8,4,4,32,256]{4,3,2,1,0:T(8,128)(2,1)}, s32[8,4,1,128]{3,2,1,0:T(1,128)}) custom-call(bf16[4,4,32,256]{3,2,1,0:T(8,128)(2,1)} %bitcast.8, s32[1,128]{1,0:T(1,128)} %get-tuple-element.16.meta), custom_call_target="tpu_custom_call" | custom-call | tf_op jit(solution)/shard_map/gather/pallas_call | solution.py:517
  69.8 7.0 %place.1 = f32[2,32,2048]{2,1,0:T(8,128)} custom-call(s32[32,128]{1,0:T(8,128)} %bitcast.9, bf16[8,16,32,256]{3,2,1,0:T(8,128)(2,1)} %bitcast.7), custom_call_target="tpu_custom_call" | custom-call | tf_op jit(solution)/shard_map/place/pallas_call | solution.py:539

commit v2 on v1

--- a/solution.py
+++ b/solution.py
@@ -18,13 +18,15 @@
 LANES = 128
 ROWS = 8
 GROUP = 4
+PIECES = 2
+VMEM_BYTES = 40 << 20
 FAR = 1 << 20
 MESH = pl.DeviceIdType.MESH
 NT = (((1,), (1,)), ((), ()))
 
 
 def dispatch_kernel(
-    slot_cap, regroup, vis, u_cell, v_cell, u_frac, v_frac, w_plane, route, taps, gain, out, table, taper, feat, dest
+    slot_cap, vis, u_cell, v_cell, u_frac, v_frac, w_plane, route, taps, gain, out, table, taper, feat, dest
 ):
     rows = vis.shape[0]
     columns = vis.shape[1]
@@ -35,16 +37,6 @@
     plane = w_plane[...] * OS
     codes = (u_cell[...], v_cell[...], plane + u_frac[...], plane + v_frac[...])
     codes = jnp.concatenate(codes, axis=0).astype(jnp.float32).astype(jnp.bfloat16)
-    if regroup:
-        count = 4 * channels
-        width = channels // GROUP
-        to = lax.broadcasted_iota(jnp.int32, (count, count), 0)
-        quarter, rest = to // (4 * width), to % (4 * width)
-        source = rest // width * channels + quarter * width + rest % width
-        turn = source == lax.broadcasted_iota(jnp.int32, (count, count), 1)
-        codes = jnp.dot(
-            jnp.where(turn, 1.0, 0.0).astype(jnp.bfloat16), codes, preferred_element_type=jnp.float32
-        ).astype(jnp.bfloat16)
     feat[pl.ds(columns, 4 * channels), :] = codes
     names = route[...]
     mine = lax.broadcasted_iota(jnp.int32, (groups, rows), 0) == names
@@ -202,53 +194,306 @@
     return parts
 
 
-def move_grid_kernel(
-    channels, send, table, taper, out, moved, total, left, right, spare, own_sem, to_sem, at_sem
+def ring(count):
+    v = lax.axis_index("vis")
+    half = count // 2
+    spot = v // 2 * (1 - v % 2) + (count - 1 - v // 2) * (v % 2)
+
+    def member(position):
+        position = (position + 2 * count) % count
+        back = position // half
+        return (1 - back) * 2 * position + back * (2 * (count - 1 - position) + 1)
+
+    return spot, member
+
+
+def prepare(slot_cap, groups, vis, codes, route, feat, dest):
+    rows, columns = vis.shape
+    feat[pl.ds(0, columns), :] = vis[...].astype(jnp.float32).T.astype(jnp.bfloat16)
+    u_cell, v_cell, u_frac, v_frac, w_plane = codes
+    channels = u_cell.shape[0]
+    plane = w_plane[...] * OS
+    codes = (u_cell[...], v_cell[...], plane + u_frac[...], plane + v_frac[...])
+    codes = jnp.concatenate(codes, axis=0).astype(jnp.float32).astype(jnp.bfloat16)
+    count = 4 * channels
+    width = channels // GROUP
+    to = lax.broadcasted_iota(jnp.int32, (count, count), 0)
+    quarter, rest = to // (4 * width), to % (4 * width)
+    source = rest // width * channels + quarter * width + rest % width
+    turn = source == lax.broadcasted_iota(jnp.int32, (count, count), 1)
+    feat[pl.ds(columns, count), :] = jnp.dot(
+        jnp.where(turn, 1.0, 0.0).astype(jnp.bfloat16), codes, preferred_element_type=jnp.float32
+    ).astype(jnp.bfloat16)
+    earlier = lax.broadcasted_iota(jnp.int32, (LANES, LANES), 0) < lax.broadcasted_iota(
+        jnp.int32, (LANES, LANES), 1
+    )
+    earlier = jnp.where(earlier, 1.0, 0.0).astype(jnp.bfloat16)
+    seen = jnp.zeros((groups, 1), jnp.float32)
+    for start in range(0, rows, LANES):
+        names = route[:, pl.ds(start, LANES)]
+        mine = lax.broadcasted_iota(jnp.int32, (groups, LANES), 0) == names
+        onehot = jnp.where(mine, 1.0, 0.0)
+        before = seen + jnp.dot(
+            onehot.astype(jnp.bfloat16), earlier, preferred_element_type=jnp.float32
+        )
+        rank = jnp.sum(onehot * before, axis=0, keepdims=True).astype(jnp.int32)
+        dest[:, pl.ds(start, LANES)] = names * slot_cap + rank
+        seen = seen + jnp.sum(onehot, axis=1, keepdims=True)
+
+
+def reduce_kernel(
+    slot_cap,
+    vis,
+    u_cell,
+    v_cell,
+    u_frac,
+    v_frac,
+    w_plane,
+    route,
+    taps,
+    gain,
+    tiles,
+    anchors,
+    out,
+    meta_out,
+    table,
+    taper,
+    feat,
+    dest,
+    left,
+    right,
+    spare,
+    partial,
+    sent,
+    landed,
+    meta,
+    meta_send,
+    meta_recv,
+    sum_send,
+    sum_recv,
+    far_send,
+    far_recv,
 ):
-    count, features, chunk = send.shape
+    count = out.shape[0]
+    rows = vis.shape[0]
+    channels = u_cell.shape[0]
+    chunk = BLK_DEV * slot_cap
     v, t = lax.axis_index("vis"), lax.axis_index("tile")
+    spot, member = ring(count)
+    sides = (1, -1)
+    each = GROUP // PIECES
+
     barrier = pltpu.get_barrier_semaphore()
     for k in range(1, count):
         pl.semaphore_signal(barrier, inc=1, device_id=((v + k) % count, t), device_id_type=MESH)
+
+    meta[...] = jnp.zeros_like(meta)
+    meta[pl.ds(0, 1), pl.ds(0, BLK_DEV)] = tiles[...]
+    meta[pl.ds(1, 2), pl.ds(0, BLK_DEV)] = anchors[...]
+    table[...] = jnp.zeros_like(table)
+    table[pl.ds(0, TAPS), :] = taps[...].astype(jnp.bfloat16).astype(jnp.float32)
+    cells = lax.broadcasted_iota(jnp.int32, (SUB, SUB * POLC), 0)
+    repeat = cells == lax.broadcasted_iota(jnp.int32, (SUB, SUB * POLC), 1) // POLC
+    taper[...] = jnp.dot(
+        gain[...],
+        jnp.where(repeat, 1.0, 0.0),
+        precision=lax.Precision.HIGHEST,
+        preferred_element_type=jnp.float32,
+    )
+    prepare(
+        slot_cap,
+        count * BLK_DEV,
+        vis,
+        (u_cell, v_cell, u_frac, v_frac, w_plane),
+        route,
+        feat,
+        dest,
+    )
     pl.semaphore_wait(barrier, count - 1)
 
-    def copy(k):
+    def tell(k):
         return pltpu.make_async_remote_copy(
-            src_ref=send.at[(v + k) % count],
-            dst_ref=moved.at[v],
-            send_sem=to_sem.at[k],
-            recv_sem=at_sem.at[k],
+            src_ref=meta,
+            dst_ref=meta_out.at[v],
+            send_sem=meta_send.at[k],
+            recv_sem=meta_recv.at[k],
             device_id=((v + k) % count, t),
             device_id_type=MESH,
         )
 
-    own = pltpu.make_async_copy(send.at[v], moved.at[v], own_sem.at[0])
-    own.start()
     for k in range(1, count):
-        copy(k).start()
-    total[...] = jnp.zeros_like(total)
-    own.wait()
-
-    def source(k, _):
-        @pl.when(k > 0)
-        def _():
-            copy(k).wait_recv()
-
-        origin = (v + count - k) % count
-
-        for piece in range(chunk // LANES):
-            features = moved[origin, :, pl.ds(piece * LANES, LANES)].astype(jnp.float32)
-            parts = grid_part(channels, features, table, left, right, spare)
-            for b, part in enumerate(parts):
-                here = pl.ds((piece * GROUP + b) * SUB, SUB)
-                total[here, :] = total[here, :] + part
+        tell(k).start()
+    meta_out[v] = meta[...]
+
+    def add(step, d, i):
+        here = (step, d, pl.ds(i * each, each))
+        return pltpu.make_async_remote_copy(
+            src_ref=sent.at[here],
+            dst_ref=landed.at[here],
+            send_sem=sum_send.at[(step * 2 + d) * PIECES + i],
+            recv_sem=sum_recv.at[(step * 2 + d) * PIECES + i],
+            device_id=(member(spot + sides[d]), t),
+            device_id_type=MESH,
+        )
+
+    def far(step, d, i):
+        ref = out.at[member(spot - sides[d] * step), pl.ds(d * GROUP + i * each, each)]
+        return pltpu.make_async_remote_copy(
+            src_ref=ref,
+            dst_ref=ref,
+            send_sem=far_send.at[(step * 2 + d) * PIECES + i],
+            recv_sem=far_recv.at[(step * 2 + d) * PIECES + i],
+            device_id=(member(spot + sides[d]), t),
+            device_id_type=MESH,
+        )
+
+    pieces = [(d, i) for i in range(PIECES) for d in range(2)]
+
+    def grid_step(step, _):
+        slots = lax.broadcasted_iota(jnp.int32, (chunk, rows), 0)
+        owner = jnp.where(slots < LANES, member(spot - 1 - step), member(spot + 1 + step))
+        pick = jnp.where(slots + owner * chunk == dest[...], 1.0, 0.0).astype(jnp.bfloat16)
+        features = lax.dot_general(feat[...], pick, NT, preferred_element_type=jnp.float32)
+        for d in range(2):
+            grids = grid_part(
+                channels, features[:, d * LANES : (d + 1) * LANES], table, left, right, spare
+            )
+            for b, part in enumerate(grids):
+                partial[d, b] = part
+        for d, i in pieces:
+            here = pl.ds(i * each, each)
+
+            @pl.when(step > 0)
+            def _():
+                add(step - 1, d, i).wait_recv()
+                partial[d, here] = partial[d, here] + landed[step - 1, d, here].astype(jnp.float32)
+
+            @pl.when(step < count - 1)
+            def _():
+                sent[step, d, here] = partial[d, here].astype(jnp.bfloat16)
+                add(step, d, i).start()
+
         return 0
 
-    lax.fori_loop(0, count, source, 0)
-    for b in range(BLK_DEV):
-        out[b] = (total[pl.ds(b * SUB, SUB), :] * taper[...]).astype(jnp.bfloat16)
+    lax.fori_loop(0, count, grid_step, 0)
+    for d, i in pieces:
+        for b in range(i * each, (i + 1) * each):
+            out[v, d * GROUP + b] = (partial[d, b] * taper[...]).astype(jnp.bfloat16)
+        far(0, d, i).start()
+
+    def forward(step, _):
+        for d, i in pieces:
+            far(step - 1, d, i).wait_recv()
+            far(step, d, i).start()
+        return 0
+
+    lax.fori_loop(1, count - 1, forward, 0)
+    for d, i in pieces:
+        far(count - 2, d, i).wait_recv()
     for k in range(1, count):
-        copy(k).wait_send()
+        tell(k).wait_recv()
+
+    def finish(step, _):
+        for d, i in pieces:
+            add(step, d, i).wait_send()
+            far(step, d, i).wait_send()
+        return 0
+
+    lax.fori_loop(0, count - 1, finish, 0)
+    for k in range(1, count):
+        tell(k).wait_send()
+
+
+def canvas_kernel(meta, subs, out, canvas):
+    v = lax.axis_index("vis")
+    tiles, height, width = out.shape
+    span = SUB * POLC
+    canvas[:, pl.ds(SUB, height), :] = jnp.zeros((tiles, height, width + LANES), jnp.float32)
+
+    def add_source(source, _):
+        for b in range(BLK_DEV):
+            tile = meta[source * ROWS, b]
+            low = meta[source * ROWS + 1, b] - v * height + SUB
+            column = meta[source * ROWS + 2, b] * POLC
+
+            @pl.when((low > 0) & (low < height + SUB))
+            def _():
+                sub = subs[source, b].astype(jnp.float32)
+                sub = jnp.concatenate([sub, jnp.zeros((SUB, LANES), jnp.float32)], axis=1)
+                sub = pltpu.roll(sub, column % LANES, 1)
+                sub = jnp.concatenate([sub, jnp.zeros((ROWS, span + LANES), jnp.float32)], axis=0)
+                sub = pltpu.roll(sub, low % ROWS, 0)
+                top = pl.multiple_of(low // ROWS * ROWS, ROWS)
+                base = pl.multiple_of(column // LANES * LANES, LANES)
+                here = (tile, pl.ds(top, SUB + ROWS), pl.ds(base, span + LANES))
+                canvas[here] = canvas[here] + sub
+
+        return 0
+
+    lax.fori_loop(0, subs.shape[0], add_source, 0)
+    out[...] = canvas[:, pl.ds(SUB, height), pl.ds(0, width)].astype(jnp.bfloat16)
+
+
+def fold_kernel(
+    canvas, own, far_out, near, middle, near_send, near_recv, far_send, far_recv
+):
+    tiles, height, width = own.shape
+    v, t = lax.axis_index("vis"), lax.axis_index("tile")
+    beside = t + 1 - 2 * (t % 2)
+    across = (t + 2) % 4
+    corner = (beside + 2) % 4
+    cut = height // 2
+    barrier = pltpu.get_barrier_semaphore()
+    for other in (beside, across):
+        pl.semaphore_signal(barrier, inc=1, device_id=(v, other), device_id_type=MESH)
+    pl.semaphore_wait(barrier, 2)
+    pieces = [(g, i) for g in range(tiles) for i in range(2)]
+
+    def to_beside(part, g, i):
+        here = pl.ds(i * cut, cut)
+        return pltpu.make_async_remote_copy(
+            src_ref=canvas.at[(corner, beside)[part] * tiles + g, here],
+            dst_ref=near.at[part, g, here],
+            send_sem=near_send.at[(part * tiles + g) * 2 + i],
+            recv_sem=near_recv.at[(part * tiles + g) * 2 + i],
+            device_id=(v, beside),
+            device_id_type=MESH,
+        )
+
+    def to_across(g, i):
+        here = pl.ds(i * cut, cut)
+        return pltpu.make_async_remote_copy(
+            src_ref=middle.at[g, here],
+            dst_ref=far_out.at[g, here],
+            send_sem=far_send.at[g * 2 + i],
+            recv_sem=far_recv.at[g * 2 + i],
+            device_id=(v, across),
+            device_id_type=MESH,
+        )
+
+    for part in range(2):
+        for g, i in pieces:
+            to_beside(part, g, i).start()
+    for g, i in pieces:
+        here = pl.ds(i * cut, cut)
+        to_beside(0, g, i).wait_recv()
+        middle[g, here] = (
+            canvas[across * tiles + g, here].astype(jnp.float32)
+            + near[0, g, here].astype(jnp.float32)
+        ).astype(jnp.bfloat16)
+        to_across(g, i).start()
+    for g, i in pieces:
+        here = pl.ds(i * cut, cut)
+        to_beside(1, g, i).wait_recv()
+        own[g, here] = canvas[t * tiles + g, here].astype(jnp.float32) + near[1, g, here].astype(
+            jnp.float32
+        )
+    for g, i in pieces:
+        to_across(g, i).wait_recv()
+    for g, i in pieces:
+        for part in range(2):
+            to_beside(part, g, i).wait_send()
+        to_across(g, i).wait_send()
 
 
 def slot_kernel(tiles, anchors, subs, out, meta):
@@ -429,15 +674,107 @@
     channels = u_cell.shape[0]
     slot_cap = max(2, 2 * rows // (BLK_DEV * vis_count))
     chunk = BLK_DEV * slot_cap
-    grouped = slot_cap * GROUP == LANES and channels % GROUP == 0
+    grouped = (
+        slot_cap * GROUP == LANES
+        and channels % GROUP == 0
+        and vis_count % 2 == 0
+        and tile_width == 4
+        and TS // vis_count % 32 == 0
+    )
     features = columns + 4 * channels
     per_owner = gt_dev * SCAP
     slots = tile_width * per_owner
     height = TS // vis_count
     width = TS * POLC
 
+    vmem = pl.BlockSpec(memory_space=pltpu.VMEM)
+    if grouped:
+        stages = vis_count - 1
+        lots = stages * 2 * PIECES
+        block = (SUB, SUB * POLC)
+        lanes = channels // GROUP * LANES
+        subs, meta = pl.pallas_call(
+            functools.partial(reduce_kernel, slot_cap),
+            in_specs=[vmem] * 11,
+            out_specs=[vmem] * 2,
+            out_shape=[
+                jax.ShapeDtypeStruct((vis_count, BLK_DEV) + block, jnp.bfloat16),
+                jax.ShapeDtypeStruct((vis_count, ROWS, LANES), jnp.int32),
+            ],
+            scratch_shapes=[
+                pltpu.VMEM((ROWS, LANES), jnp.float32),
+                pltpu.VMEM(block, jnp.float32),
+                pltpu.VMEM((features, rows), jnp.bfloat16),
+                pltpu.VMEM((1, rows), jnp.int32),
+                pltpu.VMEM((GROUP, SUB, lanes), jnp.bfloat16),
+                pltpu.VMEM((GROUP, SUB * POLC, lanes), jnp.bfloat16),
+                pltpu.VMEM((channels // GROUP, SUB, LANES), jnp.float32),
+                pltpu.VMEM((2, GROUP) + block, jnp.float32),
+                pltpu.VMEM((stages, 2, GROUP) + block, jnp.bfloat16),
+                pltpu.VMEM((stages, 2, GROUP) + block, jnp.bfloat16),
+                pltpu.VMEM((ROWS, LANES), jnp.int32),
+                pltpu.SemaphoreType.DMA((vis_count,)),
+                pltpu.SemaphoreType.DMA((vis_count,)),
+            ]
+            + [pltpu.SemaphoreType.DMA((lots,))] * 4,
+            compiler_params=pltpu.CompilerParams(
+                collective_id=1, has_side_effects=True, vmem_limit_bytes=VMEM_BYTES
+            ),
+            name="reduce",
+        )(
+            vis_data,
+            u_cell,
+            v_cell,
+            u_frac,
+            v_frac,
+            w_plane,
+            block_route.reshape(1, rows),
+            kernel_taps.T,
+            taper_gain,
+            sub_tile.reshape(1, BLK_DEV),
+            sub_anchor.T,
+        )
+        canvas = pl.pallas_call(
+            canvas_kernel,
+            grid_spec=pltpu.PrefetchScalarGridSpec(
+                num_scalar_prefetch=1,
+                grid=(1,),
+                in_specs=[vmem],
+                out_specs=vmem,
+                scratch_shapes=[
+                    pltpu.VMEM((GT, height + 2 * SUB + ROWS, width + LANES), jnp.float32),
+                ],
+            ),
+            out_shape=jax.ShapeDtypeStruct((GT, height, width), jnp.bfloat16),
+            compiler_params=pltpu.CompilerParams(vmem_limit_bytes=VMEM_BYTES),
+            name="canvas",
+        )(meta.reshape(vis_count * ROWS, LANES), subs)
+        portion = (gt_dev, height, width)
+        own, other = pl.pallas_call(
+            fold_kernel,
+            in_specs=[vmem],
+            out_specs=[vmem] * 2,
+            out_shape=[
+                jax.ShapeDtypeStruct(portion, jnp.float32),
+                jax.ShapeDtypeStruct(portion, jnp.bfloat16),
+            ],
+            scratch_shapes=[
+                pltpu.VMEM((2,) + portion, jnp.bfloat16),
+                pltpu.VMEM(portion, jnp.bfloat16),
+                pltpu.SemaphoreType.DMA((4 * gt_dev,)),
+                pltpu.SemaphoreType.DMA((4 * gt_dev,)),
+                pltpu.SemaphoreType.DMA((2 * gt_dev,)),
+                pltpu.SemaphoreType.DMA((2 * gt_dev,)),
+            ],
+            compiler_params=pltpu.CompilerParams(
+                collective_id=0, has_side_effects=True, vmem_limit_bytes=VMEM_BYTES
+            ),
+            name="fold",
+        )(canvas)
+        return own + other.astype(jnp.float32)
+
     send, table, taper = pl.pallas_call(
-        functools.partial(dispatch_kernel, slot_cap, grouped),
+        functools.partial(dispatch_kernel, slot_cap),
         out_shape=[
             jax.ShapeDtypeStruct((vis_count, features, chunk), jnp.bfloat16),
             jax.ShapeDtypeStruct((ROWS, LANES), jnp.float32),
@@ -460,48 +797,27 @@
         taper_gain,
     )
     covered = min(BLK_DEV, LANES // slot_cap)
-    vmem = pl.BlockSpec(memory_space=pltpu.VMEM)
     work = [
         pltpu.VMEM((BLK_DEV * SUB, SUB * POLC), jnp.float32),
         pltpu.VMEM((covered * SUB, channels * LANES), jnp.bfloat16),
         pltpu.VMEM((SUB * POLC, channels * LANES), jnp.bfloat16),
     ]
     gridded = jax.ShapeDtypeStruct((BLK_DEV, SUB, SUB * POLC), jnp.bfloat16)
-    if grouped:
-        subs = pl.pallas_call(
-            functools.partial(move_grid_kernel, channels),
-            in_specs=[vmem, vmem, vmem],
-            out_specs=vmem,
-            out_shape=gridded,
-            scratch_shapes=[pltpu.VMEM(send.shape, jnp.bfloat16)]
-            + [
-                work[0],
-                pltpu.VMEM((GROUP, SUB, channels // GROUP * LANES), jnp.bfloat16),
-                pltpu.VMEM((GROUP, SUB * POLC, channels // GROUP * LANES), jnp.bfloat16),
-                pltpu.VMEM((channels // GROUP, SUB, LANES), jnp.float32),
-                pltpu.SemaphoreType.DMA((1,)),
-                pltpu.SemaphoreType.DMA((vis_count,)),
-                pltpu.SemaphoreType.DMA((vis_count,)),
-            ],
-            compiler_params=pltpu.CompilerParams(collective_id=1, has_side_effects=True),
-            name="move_grid",
-        )(send, table, taper)
-    else:
-        moved = lax.all_to_all(send, "vis", split_axis=0, concat_axis=0, tiled=True)
-        moved = jnp.transpose(moved, (1, 0, 2)).reshape(1, features, vis_count * chunk)
-        subs = pl.pallas_call(
-            functools.partial(grid_kernel, slot_cap, chunk, channels),
-            grid=(moved.shape[2] // LANES,),
-            in_specs=[
-                pl.BlockSpec((1, features, LANES), lambda s: (0, 0, s)),
-                pl.BlockSpec(table.shape, lambda s: (0, 0)),
-                pl.BlockSpec(taper.shape, lambda s: (0, 0)),
-            ],
-            out_specs=pl.BlockSpec(gridded.shape, lambda s: (0, 0, 0)),
-            out_shape=gridded,
-            scratch_shapes=work,
-            name="grid",
-        )(moved, table, taper)
+    moved = lax.all_to_all(send, "vis", split_axis=0, concat_axis=0, tiled=True)
+    moved = jnp.transpose(moved, (1, 0, 2)).reshape(1, features, vis_count * chunk)
+    subs = pl.pallas_call(
+        functools.partial(grid_kernel, slot_cap, chunk, channels),
+        grid=(moved.shape[2] // LANES,),
+        in_specs=[
+            pl.BlockSpec((1, features, LANES), lambda s: (0, 0, s)),
+            pl.BlockSpec(table.shape, lambda s: (0, 0)),
+            pl.BlockSpec(taper.shape, lambda s: (0, 0)),
+        ],
+        out_specs=pl.BlockSpec(gridded.shape, lambda s: (0, 0, 0)),
+        out_shape=gridded,
+        scratch_shapes=work,
+        name="grid",
+    )(moved, table, taper)
     scalars = pl.BlockSpec(memory_space=pltpu.SMEM)
     subs, meta = pl.pallas_call(
         slot_kernel,

time: 77.3 us -> 74.1 us (0.959)
  Pallas kernels: 76.8 us -> 65.7 us
  local copies, waits for them, and re-layouts: 0 us -> 7.24 us
  other arithmetic: 0 us -> 0.84 us
    pallas_call x5 -> x3, Pallas kernels: 76.8 us -> 65.7 us  [the longest x1 52.5 us: on_device(): pl.pallas_call(functools.partial(reduce_kernel, slot_cap), in_specs=[vmem...]
    unnamed x0 -> x22, local copies, waits for them, and re-layouts: none -> 7.24 us
    add x0 -> x1, other arithmetic: none -> 0.84 us  [on_device(): return own + other.astype(jnp.float32)]
where the time goes in v2:
time: 74.1 us; the launch traced here: 73.8 us
  Pallas kernels  65.7 us (89%)
  local copies, waits for them, and re-layouts  7.24 us (10%)
  other arithmetic  0.84 us (1%)
    pallas_call x1, Pallas kernels, on_device(): pl.pallas_call(functools.partial(reduce_kernel, slot_cap), in_specs=[vmem...  52.5 us
    pallas_call x1, Pallas kernels, on_device(): pl.pallas_call(fold_kernel, in_specs=[vmem], out_specs=[vmem] * 2, out_sh...  10 us
    unnamed x22, local copies, waits for them, and re-layouts  7.24 us
    pallas_call x1, Pallas kernels, on_device(): pl.pallas_call(canvas_kernel, grid_spec=pltpu.PrefetchScalarGridSpec(num_...  3.2 us

profile of v2, /device:TPU:0, one launch (start us, length us, event | category | flops | bytes accessed | tf_op | source)
XLA Modules:
  0.0 73.8 jit_solution(4612298811322342331)
XLA Ops:
  0.0 0.0 copy-start.7
  0.0 0.0 copy-start.9
  0.0 0.0 copy-start.10
  0.0 0.7 copy-done.7
  0.7 0.0 copy-done.9
  0.7 0.0 copy-done.10
  0.7 0.0 copy-start
  0.7 0.9 %copy-done = bf16[1024,128]{1,0:T(8,128)(2,1)S(1)} copy-done((bf16[1024,128]{1,0:T(8,128)(2,1)S(1)}, bf16[1024,128]{1,0:T(8,128)(2,1)}, u32[]{:S(2)}) %copy-start) | copy-done | bytes 262168
  1.6 0.0 copy-start.1
  1.7 0.8 %copy-done.1 = s32[16,1024]{1,0:T(8,128)S(1)} copy-done((s32[16,1024]{1,0:T(8,128)S(1)}, s32[16,1024]{1,0:T(8,128)}, u32[]{:S(2)}) %copy-start.1) | copy-done | bytes 65560
  2.5 0.0 copy-start.2
  2.5 0.8 %copy-done.2 = s32[16,1024]{1,0:T(8,128)S(1)} copy-done((s32[16,1024]{1,0:T(8,128)S(1)}, s32[16,1024]{1,0:T(8,128)}, u32[]{:S(2)}) %copy-start.2) | copy-done | bytes 65560
  3.3 0.0 copy-start.3
  3.3 0.8 %copy-done.3 = s32[16,1024]{1,0:T(8,128)S(1)} copy-done((s32[16,1024]{1,0:T(8,128)S(1)}, s32[16,1024]{1,0:T(8,128)}, u32[]{:S(2)}) %copy-start.3) | copy-done | bytes 65560
  4.2 0.0 copy-start.4
  4.2 0.8 %copy-done.4 = s32[16,1024]{1,0:T(8,128)S(1)} copy-done((s32[16,1024]{1,0:T(8,128)S(1)}, s32[16,1024]{1,0:T(8,128)}, u32[]{:S(2)}) %copy-start.4) | copy-done | bytes 65560
  5.0 0.0 copy-start.5
  5.0 0.8 %copy-done.5 = s32[16,1024]{1,0:T(8,128)S(1)} copy-done((s32[16,1024]{1,0:T(8,128)S(1)}, s32[16,1024]{1,0:T(8,128)}, u32[]{:S(2)}) %copy-start.5) | copy-done | bytes 65560
  5.8 0.0 copy-start.6
  5.9 0.7 copy-done.6
  6.6 0.0 copy-start.8
  6.6 0.7 copy-done.8
  7.3 52.5 %reduce.1 = (bf16[8,8,32,256]{3,2,1,0:T(8,128)(2,1)S(1)}, s32[8,8,128]{2,1,0:T(8,128)S(1)}) custom-call(bf16[1024,128]{1,0:T(8,128)(2,1)S(1)} %copy-done, s32[16,1024]{1,0:T(8,128)S(1)} %copy-done.1, s32[16,1024]{1,0:T(8,128)S(1)} %copy-done.2, s32[16,1024]{1,0:T(8,128)S(1)} %copy-done.3, s32[16,1024]{1,0:T(8,128)S(1)} %copy-done.4, ...), custom_call_target="tpu_custom_call" | custom-call | tf_op jit(solution)/shard_map/reduce/pallas_call | solution.py:696
  59.8 3.2 %canvas.1 = bf16[8,32,2048]{2,1,0:T(8,128)(2,1)S(1)} custom-call(s32[64,128]{1,0:T(8,128)S(1)} %bitcast.5, bf16[8,8,32,256]{3,2,1,0:T(8,128)(2,1)S(1)} %get-tuple-element.10.subs), custom_call_target="tpu_custom_call" | custom-call | tf_op jit(solution)/shard_map/canvas/pallas_call | solution.py:737
  63.0 10.0 %fold.1 = (f32[2,32,2048]{2,1,0:T(8,128)S(1)}, bf16[2,32,2048]{2,1,0:T(8,128)(2,1)S(1)}) custom-call(bf16[8,32,2048]{2,1,0:T(8,128)(2,1)S(1)} %canvas.1), custom_call_target="tpu_custom_call" | custom-call | tf_op jit(solution)/shard_map/fold/pallas_call | solution.py:753
  73.0 0.8 %convert_add_fusion = f32[2,32,2048]{2,1,0:T(8,128)} fusion(f32[2,32,2048]{2,1,0:T(8,128)S(1)} %get-tuple-element.11, bf16[2,32,2048]{2,1,0:T(8,128)(2,1)S(1)} %get-tuple-element.12), kind=kLoop, calls=%fused_computation | loop fusion | flops 262144 | bytes 1310720 | tf_op jit(solution)/shard_map/add | solution.py:774
Async XLA Ops:
  0.0 0.7 copy-start.7
  0.0 0.7 copy-start.9
  0.0 0.7 copy-start.10
  0.7 1.0 %copy-start = (bf16[1024,128]{1,0:T(8,128)(2,1)S(1)}, bf16[1024,128]{1,0:T(8,128)(2,1)}, u32[]{:S(2)}) copy-start(bf16[1024,128]{1,0:T(8,128)(2,1)} %vis.1) | copy-start | bytes 786436
  1.6 0.8 %copy-start.1 = (s32[16,1024]{1,0:T(8,128)S(1)}, s32[16,1024]{1,0:T(8,128)}, u32[]{:S(2)}) copy-start(s32[16,1024]{1,0:T(8,128)} %u_cell.1) | copy-start | bytes 196612
  2.5 0.8 %copy-start.2 = (s32[16,1024]{1,0:T(8,128)S(1)}, s32[16,1024]{1,0:T(8,128)}, u32[]{:S(2)}) copy-start(s32[16,1024]{1,0:T(8,128)} %v_cell.1) | copy-start | bytes 196612
  3.3 0.8 %copy-start.3 = (s32[16,1024]{1,0:T(8,128)S(1)}, s32[16,1024]{1,0:T(8,128)}, u32[]{:S(2)}) copy-start(s32[16,1024]{1,0:T(8,128)} %u_frac.1) | copy-start | bytes 196612
  4.2 0.8 %copy-start.4 = (s32[16,1024]{1,0:T(8,128)S(1)}, s32[16,1024]{1,0:T(8,128)}, u32[]{:S(2)}) copy-start(s32[16,1024]{1,0:T(8,128)} %v_frac.1) | copy-start | bytes 196612
  5.0 0.8 %copy-start.5 = (s32[16,1024]{1,0:T(8,128)S(1)}, s32[16,1024]{1,0:T(8,128)}, u32[]{:S(2)}) copy-start(s32[16,1024]{1,0:T(8,128)} %w_plane.1) | copy-start | bytes 196612
  5.8 0.7 copy-start.6
  6.6 0.7 copy-start.8

commit v3 on v2

--- a/solution.py
+++ b/solution.py
@@ -18,8 +18,8 @@
 LANES = 128
 ROWS = 8
 GROUP = 4
-PIECES = 2
-VMEM_BYTES = 40 << 20
+PIECES = 4
+VMEM_BYTES = 24 << 20
 FAR = 1 << 20
 MESH = pl.DeviceIdType.MESH
 NT = (((1,), (1,)), ((), ()))
@@ -194,19 +194,6 @@
     return parts
 
 
-def ring(count):
-    v = lax.axis_index("vis")
-    half = count // 2
-    spot = v // 2 * (1 - v % 2) + (count - 1 - v // 2) * (v % 2)
-
-    def member(position):
-        position = (position + 2 * count) % count
-        back = position // half
-        return (1 - back) * 2 * position + back * (2 * (count - 1 - position) + 1)
-
-    return spot, member
-
-
 def prepare(slot_cap, groups, vis, codes, route, feat, dest):
     rows, columns = vis.shape
     feat[pl.ds(0, columns), :] = vis[...].astype(jnp.float32).T.astype(jnp.bfloat16)
@@ -243,6 +230,19 @@
 
 def reduce_kernel(
     slot_cap,
+    vis_hbm,
+    u_cell_hbm,
+    v_cell_hbm,
+    u_frac_hbm,
+    v_frac_hbm,
+    w_plane_hbm,
+    route_hbm,
+    taps_hbm,
+    gain_hbm,
+    tiles_hbm,
+    anchors_hbm,
+    out,
+    meta_out,
     vis,
     u_cell,
     v_cell,
@@ -254,8 +254,6 @@
     gain,
     tiles,
     anchors,
-    out,
-    meta_out,
     table,
     taper,
     feat,
@@ -264,33 +262,59 @@
     right,
     spare,
     partial,
-    sent,
-    landed,
+    x_sent,
+    x_landed,
+    z_sent,
+    z_landed,
     meta,
+    in_sem,
     meta_send,
     meta_recv,
-    sum_send,
-    sum_recv,
-    far_send,
-    far_recv,
+    x_send,
+    x_recv,
+    z_send,
+    z_recv,
+    to_z_send,
+    to_z_recv,
+    to_x_send,
+    to_x_recv,
 ):
     count = out.shape[0]
+    height = count // 2
     rows = vis.shape[0]
     channels = u_cell.shape[0]
     chunk = BLK_DEV * slot_cap
     v, t = lax.axis_index("vis"), lax.axis_index("tile")
-    spot, member = ring(count)
-    sides = (1, -1)
-    each = GROUP // PIECES
+    z, x = v // 2, v % 2
+    each = BLK_DEV // PIECES
+    remote = functools.partial(pltpu.make_async_remote_copy, device_id_type=MESH)
 
     barrier = pltpu.get_barrier_semaphore()
     for k in range(1, count):
         pl.semaphore_signal(barrier, inc=1, device_id=((v + k) % count, t), device_id_type=MESH)
-
+    pairs = (
+        (vis_hbm, vis),
+        (u_cell_hbm, u_cell),
+        (v_cell_hbm, v_cell),
+        (u_frac_hbm, u_frac),
+        (v_frac_hbm, v_frac),
+        (w_plane_hbm, w_plane),
+        (route_hbm, route),
+        (taps_hbm, taps),
+        (gain_hbm, gain),
+        (tiles_hbm, tiles),
+        (anchors_hbm, anchors),
+    )
+    loads = [pltpu.make_async_copy(src, dst, in_sem.at[i]) for i, (src, dst) in enumerate(pairs)]
+    for load in loads:
+        load.start()
     meta[...] = jnp.zeros_like(meta)
+    table[...] = jnp.zeros_like(table)
+    for load in loads:
+        load.wait()
+
     meta[pl.ds(0, 1), pl.ds(0, BLK_DEV)] = tiles[...]
     meta[pl.ds(1, 2), pl.ds(0, BLK_DEV)] = anchors[...]
-    table[...] = jnp.zeros_like(table)
     table[pl.ds(0, TAPS), :] = taps[...].astype(jnp.bfloat16).astype(jnp.float32)
     cells = lax.broadcasted_iota(jnp.int32, (SUB, SUB * POLC), 0)
     repeat = cells == lax.broadcasted_iota(jnp.int32, (SUB, SUB * POLC), 1) // POLC
@@ -311,97 +335,121 @@
     )
     pl.semaphore_wait(barrier, count - 1)
 
+    def piece(i):
+        return pl.ds(i * each, each)
+
     def tell(k):
-        return pltpu.make_async_remote_copy(
+        return remote(
             src_ref=meta,
             dst_ref=meta_out.at[v],
             send_sem=meta_send.at[k],
             recv_sem=meta_recv.at[k],
             device_id=((v + k) % count, t),
-            device_id_type=MESH,
+        )
+
+    def add_x(j, i):
+        return remote(
+            src_ref=x_sent.at[j, piece(i)],
+            dst_ref=x_landed.at[j, piece(i)],
+            send_sem=x_send.at[j * PIECES + i],
+            recv_sem=x_recv.at[j * PIECES + i],
+            device_id=(z * 2 + 1 - x, t),
+        )
+
+    def add_z(j, i):
+        return remote(
+            src_ref=z_sent.at[j - 1, piece(i)],
+            dst_ref=z_landed.at[j - 1, piece(i)],
+            send_sem=z_send.at[(j - 1) * PIECES + i],
+            recv_sem=z_recv.at[(j - 1) * PIECES + i],
+            device_id=((z + j) % height * 2 + x, t),
+        )
+
+    def give_z(j, i):
+        return remote(
+            src_ref=out.at[v, piece(i)],
+            dst_ref=out.at[v, piece(i)],
+            send_sem=to_z_send.at[(j - 1) * PIECES + i],
+            recv_sem=to_z_recv.at[(j - 1) * PIECES + i],
+            device_id=((z + j) % height * 2 + x, t),
+        )
+
+    def give_x(j, i):
+        ref = out.at[(z + height - j) % height * 2 + x, piece(i)]
+        return remote(
+            src_ref=ref,
+            dst_ref=ref,
+            send_sem=to_x_send.at[j * PIECES + i],
+            recv_sem=to_x_recv.at[j * PIECES + i],
+            device_id=(z * 2 + 1 - x, t),
         )
 
     for k in range(1, count):
         tell(k).start()
     meta_out[v] = meta[...]
 
-    def add(step, d, i):
-        here = (step, d, pl.ds(i * each, each))
-        return pltpu.make_async_remote_copy(
-            src_ref=sent.at[here],
-            dst_ref=landed.at[here],
-            send_sem=sum_send.at[(step * 2 + d) * PIECES + i],
-            recv_sem=sum_recv.at[(step * 2 + d) * PIECES + i],
-            device_id=(member(spot + sides[d]), t),
-            device_id_type=MESH,
-        )
-
-    def far(step, d, i):
-        ref = out.at[member(spot - sides[d] * step), pl.ds(d * GROUP + i * each, each)]
-        return pltpu.make_async_remote_copy(
-            src_ref=ref,
-            dst_ref=ref,
-            send_sem=far_send.at[(step * 2 + d) * PIECES + i],
-            recv_sem=far_recv.at[(step * 2 + d) * PIECES + i],
-            device_id=(member(spot + sides[d]), t),
-            device_id_type=MESH,
-        )
-
-    pieces = [(d, i) for i in range(PIECES) for d in range(2)]
-
     def grid_step(step, _):
-        slots = lax.broadcasted_iota(jnp.int32, (chunk, rows), 0)
-        owner = jnp.where(slots < LANES, member(spot - 1 - step), member(spot + 1 + step))
-        pick = jnp.where(slots + owner * chunk == dest[...], 1.0, 0.0).astype(jnp.bfloat16)
+        last = step == count - 1
+        mine = jnp.logical_or(jnp.logical_and(step > 0, step % 2 == 0), last)
+        j = jnp.where(last, 0, jnp.where(mine, step // 2, (step + 3) // 2 % height))
+        owner = (z + j) % height * 2 + jnp.where(mine, x, 1 - x)
+        slots = lax.broadcasted_iota(jnp.int32, (chunk, rows), 0) + owner * chunk
+        pick = jnp.where(slots == dest[...], 1.0, 0.0).astype(jnp.bfloat16)
         features = lax.dot_general(feat[...], pick, NT, preferred_element_type=jnp.float32)
-        for d in range(2):
+        for d in range(chunk // LANES):
             grids = grid_part(
                 channels, features[:, d * LANES : (d + 1) * LANES], table, left, right, spare
             )
             for b, part in enumerate(grids):
-                partial[d, b] = part
-        for d, i in pieces:
-            here = pl.ds(i * each, each)
-
-            @pl.when(step > 0)
-            def _():
-                add(step - 1, d, i).wait_recv()
-                partial[d, here] = partial[d, here] + landed[step - 1, d, here].astype(jnp.float32)
-
-            @pl.when(step < count - 1)
-            def _():
-                sent[step, d, here] = partial[d, here].astype(jnp.bfloat16)
-                add(step, d, i).start()
+                partial[d * GROUP + b] = part
+
+        @pl.when(jnp.logical_not(mine))
+        def _():
+            for i in range(PIECES):
+                x_sent[j, piece(i)] = partial[piece(i)].astype(jnp.bfloat16)
+                add_x(j, i).start()
+
+        @pl.when(mine)
+        def _():
+            for i in range(PIECES):
+                add_x(j, i).wait_recv()
+                partial[piece(i)] = partial[piece(i)] + x_landed[j, piece(i)].astype(jnp.float32)
+
+                @pl.when(j > 0)
+                def _():
+                    z_sent[j - 1, piece(i)] = partial[piece(i)].astype(jnp.bfloat16)
+                    add_z(j, i).start()
 
         return 0
 
     lax.fori_loop(0, count, grid_step, 0)
-    for d, i in pieces:
-        for b in range(i * each, (i + 1) * each):
-            out[v, d * GROUP + b] = (partial[d, b] * taper[...]).astype(jnp.bfloat16)
-        far(0, d, i).start()
-
-    def forward(step, _):
-        for d, i in pieces:
-            far(step - 1, d, i).wait_recv()
-            far(step, d, i).start()
-        return 0
-
-    lax.fori_loop(1, count - 1, forward, 0)
-    for d, i in pieces:
-        far(count - 2, d, i).wait_recv()
+    for i in range(PIECES):
+        whole = partial[piece(i)]
+        for j in range(1, height):
+            add_z(j, i).wait_recv()
+            whole = whole + z_landed[j - 1, piece(i)].astype(jnp.float32)
+        out[v, piece(i)] = (whole * taper[...][None]).astype(jnp.bfloat16)
+        for j in range(1, height):
+            give_z(j, i).start()
+        give_x(0, i).start()
+    for i in range(PIECES):
+        for j in range(1, height):
+            give_z(j, i).wait_recv()
+            give_x(j, i).start()
+    for i in range(PIECES):
+        for j in range(height):
+            give_x(j, i).wait_recv()
     for k in range(1, count):
         tell(k).wait_recv()
-
-    def finish(step, _):
-        for d, i in pieces:
-            add(step, d, i).wait_send()
-            far(step, d, i).wait_send()
-        return 0
-
-    lax.fori_loop(0, count - 1, finish, 0)
     for k in range(1, count):
         tell(k).wait_send()
+    for i in range(PIECES):
+        for j in range(height):
+            add_x(j, i).wait_send()
+            give_x(j, i).wait_send()
+        for j in range(1, height):
+            add_z(j, i).wait_send()
+            give_z(j, i).wait_send()
 
 
 def canvas_kernel(meta, subs, out, canvas):
@@ -678,6 +726,7 @@
         slot_cap * GROUP == LANES
         and channels % GROUP == 0
         and vis_count % 2 == 0
+        and vis_count > 2
         and tile_width == 4
         and TS // vis_count % 32 == 0
     )
@@ -689,39 +738,10 @@
 
     vmem = pl.BlockSpec(memory_space=pltpu.VMEM)
     if grouped:
-        stages = vis_count - 1
-        lots = stages * 2 * PIECES
+        layers = vis_count // 2
         block = (SUB, SUB * POLC)
         lanes = channels // GROUP * LANES
-        subs, meta = pl.pallas_call(
-            functools.partial(reduce_kernel, slot_cap),
-            in_specs=[vmem] * 11,
-            out_specs=[vmem] * 2,
-            out_shape=[
-                jax.ShapeDtypeStruct((vis_count, BLK_DEV) + block, jnp.bfloat16),
-                jax.ShapeDtypeStruct((vis_count, ROWS, LANES), jnp.int32),
-            ],
-            scratch_shapes=[
-                pltpu.VMEM((ROWS, LANES), jnp.float32),
-                pltpu.VMEM(block, jnp.float32),
-                pltpu.VMEM((features, rows), jnp.bfloat16),
-                pltpu.VMEM((1, rows), jnp.int32),
-                pltpu.VMEM((GROUP, SUB, lanes), jnp.bfloat16),
-                pltpu.VMEM((GROUP, SUB * POLC, lanes), jnp.bfloat16),
-                pltpu.VMEM((channels // GROUP, SUB, LANES), jnp.float32),
-                pltpu.VMEM((2, GROUP) + block, jnp.float32),
-                pltpu.VMEM((stages, 2, GROUP) + block, jnp.bfloat16),
-                pltpu.VMEM((stages, 2, GROUP) + block, jnp.bfloat16),
-                pltpu.VMEM((ROWS, LANES), jnp.int32),
-                pltpu.SemaphoreType.DMA((vis_count,)),
-                pltpu.SemaphoreType.DMA((vis_count,)),
-            ]
-            + [pltpu.SemaphoreType.DMA((lots,))] * 4,
-            compiler_params=pltpu.CompilerParams(
-                collective_id=1, has_side_effects=True, vmem_limit_bytes=VMEM_BYTES
-            ),
-            name="reduce",
-        )(
+        operands = (
             vis_data,
             u_cell,
             v_cell,
@@ -734,6 +754,43 @@
             sub_tile.reshape(1, BLK_DEV),
             sub_anchor.T,
         )
+        subs, meta = pl.pallas_call(
+            functools.partial(reduce_kernel, slot_cap),
+            in_specs=[pl.BlockSpec(memory_space=pltpu.HBM)] * len(operands),
+            out_specs=[vmem] * 2,
+            out_shape=[
+                jax.ShapeDtypeStruct((vis_count, BLK_DEV) + block, jnp.bfloat16),
+                jax.ShapeDtypeStruct((vis_count, ROWS, LANES), jnp.int32),
+            ],
+            scratch_shapes=[pltpu.VMEM(operand.shape, operand.dtype) for operand in operands]
+            + [
+                pltpu.VMEM((ROWS, LANES), jnp.float32),
+                pltpu.VMEM(block, jnp.float32),
+                pltpu.VMEM((features, rows), jnp.bfloat16),
+                pltpu.VMEM((1, rows), jnp.int32),
+                pltpu.VMEM((GROUP, SUB, lanes), jnp.bfloat16),
+                pltpu.VMEM((GROUP, SUB * POLC, lanes), jnp.bfloat16),
+                pltpu.VMEM((channels // GROUP, SUB, LANES), jnp.float32),
+                pltpu.VMEM((BLK_DEV,) + block, jnp.float32),
+                pltpu.VMEM((layers, BLK_DEV) + block, jnp.bfloat16),
+                pltpu.VMEM((layers, BLK_DEV) + block, jnp.bfloat16),
+                pltpu.VMEM((layers - 1, BLK_DEV) + block, jnp.bfloat16),
+                pltpu.VMEM((layers - 1, BLK_DEV) + block, jnp.bfloat16),
+                pltpu.VMEM((ROWS, LANES), jnp.int32),
+                pltpu.SemaphoreType.DMA((len(operands),)),
+            ]
+            + [
+                pltpu.SemaphoreType.DMA((lots,))
+                for lots in [vis_count] * 2
+                + [layers * PIECES] * 2
+                + [(layers - 1) * PIECES] * 4
+                + [layers * PIECES] * 2
+            ],
+            compiler_params=pltpu.CompilerParams(
+                collective_id=1, has_side_effects=True, vmem_limit_bytes=VMEM_BYTES
+            ),
+            name="reduce",
+        )(*[pltpu.with_memory_space_constraint(operand, pltpu.HBM) for operand in operands])
         canvas = pl.pallas_call(
             canvas_kernel,
             grid_spec=pltpu.PrefetchScalarGridSpec(

time: 74.1 us -> 54.6 us (0.74)
  Pallas kernels: 65.7 us -> 53.6 us
  local copies, waits for them, and re-layouts: 7.24 us -> 0 us
    pallas_call x1, Pallas kernels: 52.5 us -> 40.7 us  [on_device(): pl.pallas_call(functools.partial(reduce_kernel, slot_cap), in_specs=[pl.B...]
    unnamed x22 -> x0, local copies, waits for them, and re-layouts: 7.24 us -> none
where the time goes in v3:
time: 54.6 us; the launch traced here: 54.5 us
  Pallas kernels  53.6 us (98%)
  other arithmetic  0.84 us (2%)
    pallas_call x1, Pallas kernels, on_device(): pl.pallas_call(functools.partial(reduce_kernel, slot_cap), in_specs=[pl.B...  40.7 us
    pallas_call x1, Pallas kernels, on_device(): pl.pallas_call(fold_kernel, in_specs=[vmem], out_specs=[vmem] * 2, out_sh...  10 us
    pallas_call x1, Pallas kernels, on_device(): pl.pallas_call(canvas_kernel, grid_spec=pltpu.PrefetchScalarGridSpec(num_...  2.91 us

profile of v3, /device:TPU:0, one launch (start us, length us, event | category | flops | bytes accessed | tf_op | source)
XLA Modules:
  0.0 54.5 jit_solution(17030529244926216908)
XLA Ops:
  0.0 40.7 %reduce.1 = (bf16[8,8,32,256]{3,2,1,0:T(8,128)(2,1)S(1)}, s32[8,8,128]{2,1,0:T(8,128)S(1)}) custom-call(bf16[1024,128]{1,0:T(8,128)(2,1)} %vis_hbm.1, s32[16,1024]{1,0:T(8,128)} %u_cell_hbm.1, s32[16,1024]{1,0:T(8,128)} %v_cell_hbm.1, s32[16,1024]{1,0:T(8,128)} %u_frac_hbm.1, s32[16,1024]{1,0:T(8,128)} %v_frac_hbm.1, s32[16,1024]{1,0:T(8,128)} %w_plane_hbm.1, ...), custom_call_target="tpu_custom_call" | custom-call | tf_op jit(solution)/shard_map/reduce/pallas_call | solution.py:757
  40.7 2.9 %canvas.1 = bf16[8,32,2048]{2,1,0:T(8,128)(2,1)S(1)} custom-call(s32[64,128]{1,0:T(8,128)S(1)} %bitcast.5, bf16[8,8,32,256]{3,2,1,0:T(8,128)(2,1)S(1)} %get-tuple-element.10.subs), custom_call_target="tpu_custom_call" | custom-call | tf_op jit(solution)/shard_map/canvas/pallas_call | solution.py:794
  43.6 10.0 %fold.1 = (f32[2,32,2048]{2,1,0:T(8,128)S(1)}, bf16[2,32,2048]{2,1,0:T(8,128)(2,1)S(1)}) custom-call(bf16[8,32,2048]{2,1,0:T(8,128)(2,1)S(1)} %canvas.1), custom_call_target="tpu_custom_call" | custom-call | tf_op jit(solution)/shard_map/fold/pallas_call | solution.py:810
  53.7 0.8 %convert_add_fusion = f32[2,32,2048]{2,1,0:T(8,128)} fusion(f32[2,32,2048]{2,1,0:T(8,128)S(1)} %get-tuple-element.11, bf16[2,32,2048]{2,1,0:T(8,128)(2,1)S(1)} %get-tuple-element.12), kind=kLoop, calls=%fused_computation | loop fusion | flops 262144 | bytes 1310720 | tf_op jit(solution)/shard_map/add | solution.py:831

commit v4 on v3

--- a/solution.py
+++ b/solution.py
@@ -258,6 +258,7 @@
     taper,
     feat,
     dest,
+    ordered,
     left,
     right,
     spare,
@@ -365,17 +366,18 @@
             device_id=((z + j) % height * 2 + x, t),
         )
 
-    def give_z(j, i):
+    def hand_z(source, side, i):
+        ref = out.at[source * 2 + x, piece(i)]
         return remote(
-            src_ref=out.at[v, piece(i)],
-            dst_ref=out.at[v, piece(i)],
-            send_sem=to_z_send.at[(j - 1) * PIECES + i],
-            recv_sem=to_z_recv.at[(j - 1) * PIECES + i],
-            device_id=((z + j) % height * 2 + x, t),
+            src_ref=ref,
+            dst_ref=ref,
+            send_sem=to_z_send.at[((1 + side) // 2 * height + source) * PIECES + i],
+            recv_sem=to_z_recv.at[source * PIECES + i],
+            device_id=((z + side) * 2 + x, t),
         )
 
     def give_x(j, i):
-        ref = out.at[(z + height - j) % height * 2 + x, piece(i)]
+        ref = out.at[j * 2 + x, piece(i)]
         return remote(
             src_ref=ref,
             dst_ref=ref,
@@ -388,18 +390,28 @@
         tell(k).start()
     meta_out[v] = meta[...]
 
-    def grid_step(step, _):
+    cells = lax.broadcasted_iota(jnp.int32, (chunk, rows), 0).astype(jnp.float32)
+    cells = cells.astype(jnp.bfloat16)
+
+    def plan(step):
         last = step == count - 1
         mine = jnp.logical_or(jnp.logical_and(step > 0, step % 2 == 0), last)
         j = jnp.where(last, 0, jnp.where(mine, step // 2, (step + 3) // 2 % height))
+        return mine, j
+
+    def sort(step, slot):
+        mine, j = plan(step)
         owner = (z + j) % height * 2 + jnp.where(mine, x, 1 - x)
-        slots = lax.broadcasted_iota(jnp.int32, (chunk, rows), 0) + owner * chunk
-        pick = jnp.where(slots == dest[...], 1.0, 0.0).astype(jnp.bfloat16)
-        features = lax.dot_general(feat[...], pick, NT, preferred_element_type=jnp.float32)
+        slots = jnp.clip(dest[...] - owner * chunk, -1, chunk).astype(jnp.float32)
+        pick = jnp.where(cells == slots.astype(jnp.bfloat16), 1.0, 0.0).astype(jnp.bfloat16)
+        ordered[slot] = lax.dot_general(feat[...], pick, NT, preferred_element_type=jnp.float32)
+
+    def grid_step(step, slot):
+        mine, j = plan(step)
+        sort(step + 1, 1 - slot)
         for d in range(chunk // LANES):
-            grids = grid_part(
-                channels, features[:, d * LANES : (d + 1) * LANES], table, left, right, spare
-            )
+            features = ordered[slot, :, pl.ds(d * LANES, LANES)]
+            grids = grid_part(channels, features, table, left, right, spare)
             for b, part in enumerate(grids):
                 partial[d * GROUP + b] = part
 
@@ -420,22 +432,42 @@
                     z_sent[j - 1, piece(i)] = partial[piece(i)].astype(jnp.bfloat16)
                     add_z(j, i).start()
 
+    def two_steps(half, _):
+        grid_step(2 * half, 0)
+        grid_step(2 * half + 1, 1)
         return 0
 
-    lax.fori_loop(0, count, grid_step, 0)
+    sort(0, 0)
+    lax.fori_loop(0, height, two_steps, 0)
     for i in range(PIECES):
         whole = partial[piece(i)]
         for j in range(1, height):
             add_z(j, i).wait_recv()
             whole = whole + z_landed[j - 1, piece(i)].astype(jnp.float32)
         out[v, piece(i)] = (whole * taper[...][None]).astype(jnp.bfloat16)
-        for j in range(1, height):
-            give_z(j, i).start()
-        give_x(0, i).start()
-    for i in range(PIECES):
-        for j in range(1, height):
-            give_z(j, i).wait_recv()
-            give_x(j, i).start()
+        @pl.when(z > 0)
+        def _():
+            hand_z(z, -1, i).start()
+
+        @pl.when(z < height - 1)
+        def _():
+            hand_z(z, 1, i).start()
+
+        give_x(z, i).start()
+    for gap in range(1, height):
+        for i in range(PIECES):
+            for side in (1, -1):
+                origin = z - side * gap
+
+                @pl.when((origin >= 0) & (origin < height))
+                def _():
+                    hand_z(origin, side, i).wait_recv()
+                    give_x(origin, i).start()
+
+                    @pl.when((z + side >= 0) & (z + side < height))
+                    def _():
+                        hand_z(origin, side, i).start()
+
     for i in range(PIECES):
         for j in range(height):
             give_x(j, i).wait_recv()
@@ -449,7 +481,15 @@
             give_x(j, i).wait_send()
         for j in range(1, height):
             add_z(j, i).wait_send()
-            give_z(j, i).wait_send()
+        for j in range(height):
+
+            @pl.when((j <= z) & (z < height - 1))
+            def _():
+                hand_z(j, 1, i).wait_send()
+
+            @pl.when((j >= z) & (z > 0))
+            def _():
+                hand_z(j, -1, i).wait_send()
 
 
 def canvas_kernel(meta, subs, out, canvas):
@@ -768,6 +808,7 @@
                 pltpu.VMEM(block, jnp.float32),
                 pltpu.VMEM((features, rows), jnp.bfloat16),
                 pltpu.VMEM((1, rows), jnp.int32),
+                pltpu.VMEM((2, features, chunk), jnp.float32),
                 pltpu.VMEM((GROUP, SUB, lanes), jnp.bfloat16),
                 pltpu.VMEM((GROUP, SUB * POLC, lanes), jnp.bfloat16),
                 pltpu.VMEM((channels // GROUP, SUB, LANES), jnp.float32),
@@ -783,8 +824,9 @@
                 pltpu.SemaphoreType.DMA((lots,))
                 for lots in [vis_count] * 2
                 + [layers * PIECES] * 2
-                + [(layers - 1) * PIECES] * 4
-                + [layers * PIECES] * 2
+                + [(layers - 1) * PIECES] * 2
+                + [2 * layers * PIECES]
+                + [layers * PIECES] * 3
             ],
             compiler_params=pltpu.CompilerParams(
                 collective_id=1, has_side_effects=True, vmem_limit_bytes=VMEM_BYTES

time: 54.6 us -> 51.9 us (0.951)
  Pallas kernels: 53.6 us -> 50.9 us
    pallas_call x1, Pallas kernels: 40.7 us -> 38.1 us  [on_device(): pl.pallas_call(functools.partial(reduce_kernel, slot_cap), in_specs=[pl.B...]
where the time goes in v4:
time: 51.9 us; the launch traced here: 51.8 us
  Pallas kernels  50.9 us (98%)
  other arithmetic  0.84 us (2%)
    pallas_call x1, Pallas kernels, on_device(): pl.pallas_call(functools.partial(reduce_kernel, slot_cap), in_specs=[pl.B...  38.1 us
    pallas_call x1, Pallas kernels, on_device(): pl.pallas_call(fold_kernel, in_specs=[vmem], out_specs=[vmem] * 2, out_sh...  10 us
    pallas_call x1, Pallas kernels, on_device(): pl.pallas_call(canvas_kernel, grid_spec=pltpu.PrefetchScalarGridSpec(num_...  2.72 us

profile of v4, /device:TPU:0, one launch (start us, length us, event | category | flops | bytes accessed | tf_op | source)
XLA Modules:
  0.0 51.8 jit_solution(5636243064488005997)
XLA Ops:
  0.0 38.1 %reduce.1 = (bf16[8,8,32,256]{3,2,1,0:T(8,128)(2,1)S(1)}, s32[8,8,128]{2,1,0:T(8,128)S(1)}) custom-call(bf16[1024,128]{1,0:T(8,128)(2,1)} %vis_hbm.1, s32[16,1024]{1,0:T(8,128)} %u_cell_hbm.1, s32[16,1024]{1,0:T(8,128)} %v_cell_hbm.1, s32[16,1024]{1,0:T(8,128)} %u_frac_hbm.1, s32[16,1024]{1,0:T(8,128)} %v_frac_hbm.1, s32[16,1024]{1,0:T(8,128)} %w_plane_hbm.1, ...), custom_call_target="tpu_custom_call" | custom-call | tf_op jit(solution)/shard_map/reduce/pallas_call | solution.py:797
  38.1 2.7 %canvas.1 = bf16[8,32,2048]{2,1,0:T(8,128)(2,1)S(1)} custom-call(s32[64,128]{1,0:T(8,128)S(1)} %bitcast.5, bf16[8,8,32,256]{3,2,1,0:T(8,128)(2,1)S(1)} %get-tuple-element.10.subs), custom_call_target="tpu_custom_call" | custom-call | tf_op jit(solution)/shard_map/canvas/pallas_call | solution.py:836
  40.9 10.0 %fold.1 = (f32[2,32,2048]{2,1,0:T(8,128)S(1)}, bf16[2,32,2048]{2,1,0:T(8,128)(2,1)S(1)}) custom-call(bf16[8,32,2048]{2,1,0:T(8,128)(2,1)S(1)} %canvas.1), custom_call_target="tpu_custom_call" | custom-call | tf_op jit(solution)/shard_map/fold/pallas_call | solution.py:852
  50.9 0.8 %convert_add_fusion = f32[2,32,2048]{2,1,0:T(8,128)} fusion(f32[2,32,2048]{2,1,0:T(8,128)S(1)} %get-tuple-element.11, bf16[2,32,2048]{2,1,0:T(8,128)(2,1)S(1)} %get-tuple-element.12), kind=kLoop, calls=%fused_computation | loop fusion | flops 262144 | bytes 1310720 | tf_op jit(solution)/shard_map/add | solution.py:873

commit v5 on v4

--- a/solution.py
+++ b/solution.py
@@ -19,6 +19,7 @@
 ROWS = 8
 GROUP = 4
 PIECES = 4
+LUMPS = 4
 VMEM_BYTES = 24 << 20
 FAR = 1 << 20
 MESH = pl.DeviceIdType.MESH
@@ -194,8 +195,27 @@
     return parts
 
 
-def prepare(slot_cap, groups, vis, codes, route, feat, dest):
-    rows, columns = vis.shape
+def rank_rows(slot_cap, groups, route, dest):
+    rows = route.shape[1]
+    earlier = lax.broadcasted_iota(jnp.int32, (LANES, LANES), 0) < lax.broadcasted_iota(
+        jnp.int32, (LANES, LANES), 1
+    )
+    earlier = jnp.where(earlier, 1.0, 0.0).astype(jnp.bfloat16)
+    seen = jnp.zeros((groups, 1), jnp.float32)
+    for start in range(0, rows, LANES):
+        names = route[:, pl.ds(start, LANES)]
+        mine = lax.broadcasted_iota(jnp.int32, (groups, LANES), 0) == names
+        onehot = jnp.where(mine, 1.0, 0.0)
+        before = seen + jnp.dot(
+            onehot.astype(jnp.bfloat16), earlier, preferred_element_type=jnp.float32
+        )
+        rank = jnp.sum(onehot * before, axis=0, keepdims=True).astype(jnp.int32)
+        dest[:, pl.ds(start, LANES)] = names * slot_cap + rank
+        seen = seen + jnp.sum(onehot, axis=1, keepdims=True)
+
+
+def stack_features(vis, codes, feat):
+    columns = vis.shape[1]
     feat[pl.ds(0, columns), :] = vis[...].astype(jnp.float32).T.astype(jnp.bfloat16)
     u_cell, v_cell, u_frac, v_frac, w_plane = codes
     channels = u_cell.shape[0]
@@ -211,25 +231,23 @@
     feat[pl.ds(columns, count), :] = jnp.dot(
         jnp.where(turn, 1.0, 0.0).astype(jnp.bfloat16), codes, preferred_element_type=jnp.float32
     ).astype(jnp.bfloat16)
-    earlier = lax.broadcasted_iota(jnp.int32, (LANES, LANES), 0) < lax.broadcasted_iota(
-        jnp.int32, (LANES, LANES), 1
-    )
-    earlier = jnp.where(earlier, 1.0, 0.0).astype(jnp.bfloat16)
-    seen = jnp.zeros((groups, 1), jnp.float32)
-    for start in range(0, rows, LANES):
-        names = route[:, pl.ds(start, LANES)]
-        mine = lax.broadcasted_iota(jnp.int32, (groups, LANES), 0) == names
-        onehot = jnp.where(mine, 1.0, 0.0)
-        before = seen + jnp.dot(
-            onehot.astype(jnp.bfloat16), earlier, preferred_element_type=jnp.float32
-        )
-        rank = jnp.sum(onehot * before, axis=0, keepdims=True).astype(jnp.int32)
-        dest[:, pl.ds(start, LANES)] = names * slot_cap + rank
-        seen = seen + jnp.sum(onehot, axis=1, keepdims=True)
+
+
+def placement(facts, height, v, t):
+    tiles = GT // 4
+    lanes = lax.broadcasted_iota(jnp.int32, facts.shape, 1) // BLK_DEV
+    low = facts - v * height + SUB
+    low = jnp.where((low > 0) & (low < height + SUB), low, 0)
+    group = pltpu.roll(facts, BLK_DEV, 1) // tiles
+    own = jnp.where(group == t, low, 0)
+    across = pltpu.roll(jnp.where(group == (t + 2) % 4, low, 0), 2 * BLK_DEV, 1)
+    facts = jnp.where(lanes == 0, facts % tiles, facts * POLC)
+    return jnp.where(lanes == 1, own, jnp.where(lanes == 3, across, facts))
 
 
 def reduce_kernel(
     slot_cap,
+    tile_rows,
     vis_hbm,
     u_cell_hbm,
     v_cell_hbm,
@@ -279,20 +297,27 @@
     to_z_recv,
     to_x_send,
     to_x_recv,
+    to_core_send,
+    to_core_recv,
+    pass_send,
+    pass_recv,
 ):
-    count = out.shape[0]
+    count = out.shape[1]
     height = count // 2
     rows = vis.shape[0]
     channels = u_cell.shape[0]
     chunk = BLK_DEV * slot_cap
     v, t = lax.axis_index("vis"), lax.axis_index("tile")
     z, x = v // 2, v % 2
+    c = t % 2
+    beside = t + 1 - 2 * c
     each = BLK_DEV // PIECES
     remote = functools.partial(pltpu.make_async_remote_copy, device_id_type=MESH)
 
     barrier = pltpu.get_barrier_semaphore()
     for k in range(1, count):
         pl.semaphore_signal(barrier, inc=1, device_id=((v + k) % count, t), device_id_type=MESH)
+    pl.semaphore_signal(barrier, inc=1, device_id=(v, beside), device_id_type=MESH)
     pairs = (
         (vis_hbm, vis),
         (u_cell_hbm, u_cell),
@@ -307,15 +332,19 @@
         (anchors_hbm, anchors),
     )
     loads = [pltpu.make_async_copy(src, dst, in_sem.at[i]) for i, (src, dst) in enumerate(pairs)]
+    loads = [loads[6]] + loads[:6] + loads[7:]
     for load in loads:
         load.start()
-    meta[...] = jnp.zeros_like(meta)
     table[...] = jnp.zeros_like(table)
-    for load in loads:
+
+    loads[0].wait()
+    rank_rows(slot_cap, count * BLK_DEV, route, dest)
+    for load in loads[1:]:
         load.wait()
-
-    meta[pl.ds(0, 1), pl.ds(0, BLK_DEV)] = tiles[...]
-    meta[pl.ds(1, 2), pl.ds(0, BLK_DEV)] = anchors[...]
+    stack_features(vis, (u_cell, v_cell, u_frac, v_frac, w_plane), feat)
+    rest = jnp.zeros((1, LANES - 3 * BLK_DEV), jnp.int32)
+    facts = [tiles[...], anchors[pl.ds(0, 1), :], anchors[pl.ds(1, 1), :], rest]
+    meta[...] = jnp.concatenate(facts, axis=1)
     table[pl.ds(0, TAPS), :] = taps[...].astype(jnp.bfloat16).astype(jnp.float32)
     cells = lax.broadcasted_iota(jnp.int32, (SUB, SUB * POLC), 0)
     repeat = cells == lax.broadcasted_iota(jnp.int32, (SUB, SUB * POLC), 1) // POLC
@@ -325,24 +354,18 @@
         precision=lax.Precision.HIGHEST,
         preferred_element_type=jnp.float32,
     )
-    prepare(
-        slot_cap,
-        count * BLK_DEV,
-        vis,
-        (u_cell, v_cell, u_frac, v_frac, w_plane),
-        route,
-        feat,
-        dest,
-    )
-    pl.semaphore_wait(barrier, count - 1)
+    pl.semaphore_wait(barrier, count)
 
     def piece(i):
         return pl.ds(i * each, each)
+
+    def lump(i):
+        return pl.ds(i * (BLK_DEV // LUMPS), BLK_DEV // LUMPS)
 
     def tell(k):
         return remote(
             src_ref=meta,
-            dst_ref=meta_out.at[v],
+            dst_ref=meta_out.at[c, v],
             send_sem=meta_send.at[k],
             recv_sem=meta_recv.at[k],
             device_id=((v + k) % count, t),
@@ -367,28 +390,48 @@
         )
 
     def hand_z(source, side, i):
-        ref = out.at[source * 2 + x, piece(i)]
+        ref = out.at[c, source * 2 + x, lump(i)]
         return remote(
             src_ref=ref,
             dst_ref=ref,
-            send_sem=to_z_send.at[((1 + side) // 2 * height + source) * PIECES + i],
-            recv_sem=to_z_recv.at[source * PIECES + i],
+            send_sem=to_z_send.at[((1 + side) // 2 * height + source) * LUMPS + i],
+            recv_sem=to_z_recv.at[source * LUMPS + i],
             device_id=((z + side) * 2 + x, t),
         )
 
     def give_x(j, i):
-        ref = out.at[j * 2 + x, piece(i)]
+        ref = out.at[c, j * 2 + x, lump(i)]
         return remote(
             src_ref=ref,
             dst_ref=ref,
-            send_sem=to_x_send.at[j * PIECES + i],
-            recv_sem=to_x_recv.at[j * PIECES + i],
+            send_sem=to_x_send.at[j * LUMPS + i],
+            recv_sem=to_x_recv.at[j * LUMPS + i],
             device_id=(z * 2 + 1 - x, t),
+        )
+
+    def give_core(source, column):
+        ref = out.at[c, source * 2 + column]
+        return remote(
+            src_ref=ref,
+            dst_ref=ref,
+            send_sem=to_core_send.at[source * 2 + column],
+            recv_sem=to_core_recv.at[source * 2 + column],
+            device_id=(v, beside),
+        )
+
+    def pass_meta():
+        ref = meta_out.at[c]
+        return remote(
+            src_ref=ref,
+            dst_ref=ref,
+            send_sem=pass_send.at[0],
+            recv_sem=pass_recv.at[0],
+            device_id=(v, beside),
         )
 
     for k in range(1, count):
         tell(k).start()
-    meta_out[v] = meta[...]
+    meta_out[c, v] = meta[...]
 
     cells = lax.broadcasted_iota(jnp.int32, (chunk, rows), 0).astype(jnp.float32)
     cells = cells.astype(jnp.bfloat16)
@@ -444,44 +487,70 @@
         for j in range(1, height):
             add_z(j, i).wait_recv()
             whole = whole + z_landed[j - 1, piece(i)].astype(jnp.float32)
-        out[v, piece(i)] = (whole * taper[...][None]).astype(jnp.bfloat16)
+        out[c, v, piece(i)] = (whole * taper[...][None]).astype(jnp.bfloat16)
+        if (i + 1) * LUMPS % PIECES:
+            continue
+        m = (i + 1) * LUMPS // PIECES - 1
+
         @pl.when(z > 0)
         def _():
-            hand_z(z, -1, i).start()
+            hand_z(z, -1, m).start()
 
         @pl.when(z < height - 1)
         def _():
-            hand_z(z, 1, i).start()
-
-        give_x(z, i).start()
+            hand_z(z, 1, m).start()
+
+        give_x(z, m).start()
+    give_core(z, x).start()
+    for k in range(1, count):
+        tell(k).wait_recv()
+    pass_meta().start()
     for gap in range(1, height):
-        for i in range(PIECES):
+        for i in range(LUMPS):
             for side in (1, -1):
                 origin = z - side * gap
 
                 @pl.when((origin >= 0) & (origin < height))
                 def _():
                     hand_z(origin, side, i).wait_recv()
-                    give_x(origin, i).start()
 
                     @pl.when((z + side >= 0) & (z + side < height))
                     def _():
                         hand_z(origin, side, i).start()
 
-    for i in range(PIECES):
-        for j in range(height):
-            give_x(j, i).wait_recv()
-    for k in range(1, count):
-        tell(k).wait_recv()
+                    give_x(origin, i).start()
+                    if i == LUMPS - 1:
+                        give_core(origin, x).start()
+
+    for gap in range(height):
+        for side in (1, -1)[: 1 + min(gap, 1)]:
+            origin = z - side * gap
+
+            @pl.when((origin >= 0) & (origin < height))
+            def _():
+                for i in range(LUMPS):
+                    give_x(origin, i).wait_recv()
+                give_core(origin, 1 - x).start()
+
+    for source in range(height):
+        for column in range(2):
+            give_core(source, column).wait()
+    pass_meta().wait_recv()
+    pass_meta().wait_send()
     for k in range(1, count):
         tell(k).wait_send()
+    for parity in range(2):
+        for source in range(count):
+            facts = meta_out[parity, source]
+            meta_out[parity, source] = placement(facts, tile_rows, v, t)
     for i in range(PIECES):
         for j in range(height):
             add_x(j, i).wait_send()
-            give_x(j, i).wait_send()
         for j in range(1, height):
             add_z(j, i).wait_send()
+    for i in range(LUMPS):
         for j in range(height):
+            give_x(j, i).wait_send()
 
             @pl.when((j <= z) & (z < height - 1))
             def _():
@@ -492,20 +561,18 @@
                 hand_z(j, -1, i).wait_send()
 
 
-def canvas_kernel(meta, subs, out, canvas):
-    v = lax.axis_index("vis")
+def canvas_kernel(lane, meta, subs, out, canvas):
     tiles, height, width = out.shape
     span = SUB * POLC
     canvas[:, pl.ds(SUB, height), :] = jnp.zeros((tiles, height, width + LANES), jnp.float32)
 
     def add_source(source, _):
         for b in range(BLK_DEV):
-            tile = meta[source * ROWS, b]
-            low = meta[source * ROWS + 1, b] - v * height + SUB
-            column = meta[source * ROWS + 2, b] * POLC
-
-            @pl.when((low > 0) & (low < height + SUB))
+            low = meta[source, lane + b]
+
+            @pl.when(low > 0)
             def _():
+                column = meta[source, 2 * BLK_DEV + b]
                 sub = subs[source, b].astype(jnp.float32)
                 sub = jnp.concatenate([sub, jnp.zeros((SUB, LANES), jnp.float32)], axis=1)
                 sub = pltpu.roll(sub, column % LANES, 1)
@@ -513,75 +580,13 @@
                 sub = pltpu.roll(sub, low % ROWS, 0)
                 top = pl.multiple_of(low // ROWS * ROWS, ROWS)
                 base = pl.multiple_of(column // LANES * LANES, LANES)
-                here = (tile, pl.ds(top, SUB + ROWS), pl.ds(base, span + LANES))
+                here = (meta[source, b], pl.ds(top, SUB + ROWS), pl.ds(base, span + LANES))
                 canvas[here] = canvas[here] + sub
 
         return 0
 
     lax.fori_loop(0, subs.shape[0], add_source, 0)
-    out[...] = canvas[:, pl.ds(SUB, height), pl.ds(0, width)].astype(jnp.bfloat16)
-
-
-def fold_kernel(
-    canvas, own, far_out, near, middle, near_send, near_recv, far_send, far_recv
-):
-    tiles, height, width = own.shape
-    v, t = lax.axis_index("vis"), lax.axis_index("tile")
-    beside = t + 1 - 2 * (t % 2)
-    across = (t + 2) % 4
-    corner = (beside + 2) % 4
-    cut = height // 2
-    barrier = pltpu.get_barrier_semaphore()
-    for other in (beside, across):
-        pl.semaphore_signal(barrier, inc=1, device_id=(v, other), device_id_type=MESH)
-    pl.semaphore_wait(barrier, 2)
-    pieces = [(g, i) for g in range(tiles) for i in range(2)]
-
-    def to_beside(part, g, i):
-        here = pl.ds(i * cut, cut)
-        return pltpu.make_async_remote_copy(
-            src_ref=canvas.at[(corner, beside)[part] * tiles + g, here],
-            dst_ref=near.at[part, g, here],
-            send_sem=near_send.at[(part * tiles + g) * 2 + i],
-            recv_sem=near_recv.at[(part * tiles + g) * 2 + i],
-            device_id=(v, beside),
-            device_id_type=MESH,
-        )
-
-    def to_across(g, i):
-        here = pl.ds(i * cut, cut)
-        return pltpu.make_async_remote_copy(
-            src_ref=middle.at[g, here],
-            dst_ref=far_out.at[g, here],
-            send_sem=far_send.at[g * 2 + i],
-            recv_sem=far_recv.at[g * 2 + i],
-            device_id=(v, across),
-            device_id_type=MESH,
-        )
-
-    for part in range(2):
-        for g, i in pieces:
-            to_beside(part, g, i).start()
-    for g, i in pieces:
-        here = pl.ds(i * cut, cut)
-        to_beside(0, g, i).wait_recv()
-        middle[g, here] = (
-            canvas[across * tiles + g, here].astype(jnp.float32)
-            + near[0, g, here].astype(jnp.float32)
-        ).astype(jnp.bfloat16)
-        to_across(g, i).start()
-    for g, i in pieces:
-        here = pl.ds(i * cut, cut)
-        to_beside(1, g, i).wait_recv()
-        own[g, here] = canvas[t * tiles + g, here].astype(jnp.float32) + near[1, g, here].astype(
-            jnp.float32
-        )
-    for g, i in pieces:
-        to_across(g, i).wait_recv()
-    for g, i in pieces:
-        for part in range(2):
-            to_beside(part, g, i).wait_send()
-        to_across(g, i).wait_send()
+    out[...] = canvas[:, pl.ds(SUB, height), pl.ds(0, width)].astype(out.dtype)
 
 
 def slot_kernel(tiles, anchors, subs, out, meta):
@@ -795,12 +800,12 @@
             sub_anchor.T,
         )
         subs, meta = pl.pallas_call(
-            functools.partial(reduce_kernel, slot_cap),
+            functools.partial(reduce_kernel, slot_cap, height),
             in_specs=[pl.BlockSpec(memory_space=pltpu.HBM)] * len(operands),
             out_specs=[vmem] * 2,
             out_shape=[
-                jax.ShapeDtypeStruct((vis_count, BLK_DEV) + block, jnp.bfloat16),
-                jax.ShapeDtypeStruct((vis_count, ROWS, LANES), jnp.int32),
+                jax.ShapeDtypeStruct((2, vis_count, BLK_DEV) + block, jnp.bfloat16),
+                jax.ShapeDtypeStruct((2, vis_count, 1, LANES), jnp.int32),
             ],
             scratch_shapes=[pltpu.VMEM(operand.shape, operand.dtype) for operand in operands]
             + [
@@ -817,7 +822,7 @@
                 pltpu.VMEM((layers, BLK_DEV) + block, jnp.bfloat16),
                 pltpu.VMEM((layers - 1, BLK_DEV) + block, jnp.bfloat16),
                 pltpu.VMEM((layers - 1, BLK_DEV) + block, jnp.bfloat16),
-                pltpu.VMEM((ROWS, LANES), jnp.int32),
+                pltpu.VMEM((1, LANES), jnp.int32),
                 pltpu.SemaphoreType.DMA((len(operands),)),
             ]
             + [
@@ -825,52 +830,42 @@
                 for lots in [vis_count] * 2
                 + [layers * PIECES] * 2
                 + [(layers - 1) * PIECES] * 2
-                + [2 * layers * PIECES]
-                + [layers * PIECES] * 3
+                + [2 * layers * LUMPS]
+                + [layers * LUMPS] * 3
+                + [vis_count] * 2
+                + [1] * 2
             ],
             compiler_params=pltpu.CompilerParams(
                 collective_id=1, has_side_effects=True, vmem_limit_bytes=VMEM_BYTES
             ),
             name="reduce",
         )(*[pltpu.with_memory_space_constraint(operand, pltpu.HBM) for operand in operands])
-        canvas = pl.pallas_call(
-            canvas_kernel,
-            grid_spec=pltpu.PrefetchScalarGridSpec(
-                num_scalar_prefetch=1,
-                grid=(1,),
-                in_specs=[vmem],
-                out_specs=vmem,
-                scratch_shapes=[
-                    pltpu.VMEM((GT, height + 2 * SUB + ROWS, width + LANES), jnp.float32),
-                ],
-            ),
-            out_shape=jax.ShapeDtypeStruct((GT, height, width), jnp.bfloat16),
-            compiler_params=pltpu.CompilerParams(vmem_limit_bytes=VMEM_BYTES),
-            name="canvas",
-        )(meta.reshape(vis_count * ROWS, LANES), subs)
-        portion = (gt_dev, height, width)
-        own, other = pl.pallas_call(
-            fold_kernel,
-            in_specs=[vmem],
-            out_specs=[vmem] * 2,
-            out_shape=[
-                jax.ShapeDtypeStruct(portion, jnp.float32),
-                jax.ShapeDtypeStruct(portion, jnp.bfloat16),
-            ],
-            scratch_shapes=[
-                pltpu.VMEM((2,) + portion, jnp.bfloat16),
-                pltpu.VMEM(portion, jnp.bfloat16),
-                pltpu.SemaphoreType.DMA((4 * gt_dev,)),
-                pltpu.SemaphoreType.DMA((4 * gt_dev,)),
-                pltpu.SemaphoreType.DMA((2 * gt_dev,)),
-                pltpu.SemaphoreType.DMA((2 * gt_dev,)),
-            ],
-            compiler_params=pltpu.CompilerParams(
-                collective_id=0, has_side_effects=True, vmem_limit_bytes=VMEM_BYTES
-            ),
-            name="fold",
-        )(canvas)
-        return own + other.astype(jnp.float32)
+        meta = meta.reshape(2 * vis_count, LANES)
+        subs = subs.reshape((2 * vis_count, BLK_DEV) + block)
+
+        def canvas(lane, dtype):
+            return pl.pallas_call(
+                functools.partial(canvas_kernel, lane),
+                grid_spec=pltpu.PrefetchScalarGridSpec(
+                    num_scalar_prefetch=1,
+                    grid=(1,),
+                    in_specs=[vmem],
+                    out_specs=vmem,
+                    scratch_shapes=[
+                        pltpu.VMEM((gt_dev, height + 2 * SUB + ROWS, width + LANES), jnp.float32),
+                    ],
+                ),
+                out_shape=jax.ShapeDtypeStruct((gt_dev, height, width), dtype),
+                compiler_params=pltpu.CompilerParams(vmem_limit_bytes=VMEM_BYTES),
+                cost_estimate=pl.CostEstimate(
+                    flops=GT * TS * width, bytes_accessed=8 * subs.size, transcendentals=0
+                ),
+                name="canvas",
+            )(meta, subs)
+
+        across = [(tile, (tile + 2) % tile_width) for tile in range(tile_width)]
+        other = lax.ppermute(canvas(3 * BLK_DEV, jnp.bfloat16), "tile", across)
+        return canvas(BLK_DEV, jnp.float32) + other.astype(jnp.float32)
 
     send, table, taper = pl.pallas_call(
         functools.partial(dispatch_kernel, slot_cap),

time: 51.9 us -> 51.5 us (level)
  Pallas kernels: 50.9 us -> 44.1 us
  waiting for transfers between devices: 0 us -> 4.56 us
  starting transfers between devices: 0 us -> 1.79 us
    pallas_call x3, Pallas kernels: 50.9 us -> 44.1 us  [the longest x1 39.5 us: on_device(): pl.pallas_call(functools.partial(reduce_kernel, slot_cap, height), in_spe...]
    ppermute x0 -> x1, waiting for transfers between devices: none -> 4.56 us  [on_device(): other = lax.ppermute(canvas(3 * BLK_DEV, jnp.bfloat16), 'tile', across)]
    ppermute x0 -> x1, starting transfers between devices: none -> 1.79 us  [on_device(): other = lax.ppermute(canvas(3 * BLK_DEV, jnp.bfloat16), 'tile', across)]
  transfers between devices with their start and end apart: 0 -> 1, of which waited for: 0 -> 1; matrix products, arithmetic and copies ran while one was open for 0% -> 0% of each run, Pallas kernels for 0% -> 5%
where the time goes in v5:
time: 51.5 us; the launch traced here: 51.3 us
  Pallas kernels  44.1 us (86%)
  waiting for transfers between devices  4.56 us (9%)
  starting transfers between devices  1.79 us (3%)
  other arithmetic  0.84 us (2%)
    pallas_call x1, Pallas kernels, on_device(): pl.pallas_call(functools.partial(reduce_kernel, slot_cap, height), in_spe...  39.5 us
    pallas_call x2, Pallas kernels, canvas(): pl.pallas_call(functools.partial(canvas_kernel, lane), grid_spec=pltpu.Pr...  4.64 us
    ppermute x1, waiting for transfers between devices, on_device(): other = lax.ppermute(canvas(3 * BLK_DEV, jnp.bfloat16), 'tile', across)  4.56 us
    ppermute x1, starting transfers between devices, on_device(): other = lax.ppermute(canvas(3 * BLK_DEV, jnp.bfloat16), 'tile', across)  1.79 us
  transfers between devices with their start and end apart: 1, of which 1 were waited for; matrix products, arithmetic and copies ran while one was open for 0% of the time, Pallas kernels for 5%

profile of v5, /device:TPU:0, one launch (start us, length us, event | category | flops | bytes accessed | tf_op | source)
XLA Modules:
  0.0 51.3 jit_solution(3164379622919554624)
XLA Ops:
  0.0 39.5 %reduce.1 = (bf16[2,8,8,32,256]{4,3,2,1,0:T(8,128)(2,1)S(1)}, s32[2,8,1,128]{3,2,1,0:T(1,128)S(1)}) custom-call(bf16[1024,128]{1,0:T(8,128)(2,1)} %vis_hbm.1, s32[16,1024]{1,0:T(8,128)} %u_cell_hbm.1, s32[16,1024]{1,0:T(8,128)} %v_cell_hbm.1, s32[16,1024]{1,0:T(8,128)} %u_frac_hbm.1, s32[16,1024]{1,0:T(8,128)} %v_frac_hbm.1, s32[16,1024]{1,0:T(8,128)} %w_plane_hbm.1, ...), custom_call_target="tpu_custom_call" | custom-call | tf_op jit(solution)/shard_map/reduce/pallas_call | solution.py:802
  39.5 2.2 %canvas.3 = bf16[2,32,2048]{2,1,0:T(8,128)(2,1)S(1)} custom-call(s32[16,128]{1,0:T(8,128)S(1)} %bitcast.8, bf16[16,8,32,256]{3,2,1,0:T(8,128)(2,1)S(1)} %bitcast.6), custom_call_target="tpu_custom_call" | custom-call | flops 4194304 | bytes 8388608 | tf_op jit(solution)/shard_map/canvas/pallas_call | solution.py:847
  41.6 1.8 %collective-permute-start = (bf16[2,32,2048]{2,1,0:T(8,128)(2,1)S(1)}, bf16[2,32,2048]{2,1,0:T(8,128)(2,1)S(1)}, u32[]{:S(2)}, u32[]{:S(2)}) collective-permute-start(bf16[2,32,2048]{2,1,0:T(8,128)(2,1)S(1)} %canvas.3), channel_id=1, source_target_pairs={{0,2},{1,3},{2,0},{3,1},{4,6},{5,7},{6,4},{7,5},{8,10},{9,11},{10,... | collective-permute-start | bytes 786440 | tf_op jit(solution)/shard_map/ppermute | solution.py:867
  43.4 2.5 %canvas.2 = f32[2,32,2048]{2,1,0:T(8,128)S(1)} custom-call(s32[16,128]{1,0:T(8,128)S(1)} %bitcast.9, bf16[16,8,32,256]{3,2,1,0:T(8,128)(2,1)S(1)} %bitcast.7), custom_call_target="tpu_custom_call" | custom-call | flops 4194304 | bytes 8388608 | tf_op jit(solution)/shard_map/canvas/pallas_call | solution.py:847
  45.9 4.6 %collective-permute-done = bf16[2,32,2048]{2,1,0:T(8,128)(2,1)S(1)} collective-permute-done((bf16[2,32,2048]{2,1,0:T(8,128)(2,1)S(1)}, bf16[2,32,2048]{2,1,0:T(8,128)(2,1)S(1)}, u32[]{:S(2)}, u32[]{:S(2)}) %collective-permute-start) | collective-permute-done | bytes 262176 | tf_op jit(solution)/shard_map/ppermute | solution.py:867
  50.5 0.8 %convert_add_fusion = f32[2,32,2048]{2,1,0:T(8,128)} fusion(f32[2,32,2048]{2,1,0:T(8,128)S(1)} %canvas.2, bf16[2,32,2048]{2,1,0:T(8,128)(2,1)S(1)} %collective-permute-done), kind=kLoop, calls=%fused_computation | loop fusion | flops 262144 | bytes 1310720 | tf_op jit(solution)/shard_map/add | solution.py:868
Async XLA Ops:
  41.6 8.8 %collective-permute-start = (bf16[2,32,2048]{2,1,0:T(8,128)(2,1)S(1)}, bf16[2,32,2048]{2,1,0:T(8,128)(2,1)S(1)}, u32[]{:S(2)}, u32[]{:S(2)}) collective-permute-start(bf16[2,32,2048]{2,1,0:T(8,128)(2,1)S(1)} %canvas.3), channel_id=1, source_target_pairs={{0,2},{1,3},{2,0},{3,1},{4,6},{5,7},{6,4},{7,5},{8,10},{9,11},{10,... | collective-permute-start | bytes 786440 | tf_op jit(solution)/shard_map/ppermute | solution.py:867

commit v6 on v5

--- a/solution.py
+++ b/solution.py
@@ -22,6 +22,7 @@
 LUMPS = 4
 VMEM_BYTES = 24 << 20
 FAR = 1 << 20
+FLAGS = 8
 MESH = pl.DeviceIdType.MESH
 NT = (((1,), (1,)), ((), ()))
 
@@ -238,11 +239,16 @@
     lanes = lax.broadcasted_iota(jnp.int32, facts.shape, 1) // BLK_DEV
     low = facts - v * height + SUB
     low = jnp.where((low > 0) & (low < height + SUB), low, 0)
-    group = pltpu.roll(facts, BLK_DEV, 1) // tiles
-    own = jnp.where(group == t, low, 0)
-    across = pltpu.roll(jnp.where(group == (t + 2) % 4, low, 0), 2 * BLK_DEV, 1)
-    facts = jnp.where(lanes == 0, facts % tiles, facts * POLC)
-    return jnp.where(lanes == 1, own, jnp.where(lanes == 3, across, facts))
+    tile = pltpu.roll(facts, BLK_DEV, 1)
+    placed = jnp.where(lanes == 0, facts % tiles, facts * POLC)
+    placed = jnp.where(lanes == 1, jnp.where(tile // tiles == t, low, 0), placed)
+    for g in range(tiles):
+        across = jnp.where(tile == (t + 2) % 4 * tiles + g, low, 0)
+        placed = jnp.where(lanes == 3 + g, pltpu.roll(across, (2 + g) * BLK_DEV, 1), placed)
+    for kind in (1, *range(3, 3 + tiles)):
+        some = jnp.max(jnp.where(lanes == kind, placed, 0), axis=1, keepdims=True)
+        placed = jnp.where(lanes == FLAGS + kind, some, placed)
+    return placed
 
 
 def reduce_kernel(
@@ -314,10 +320,6 @@
     each = BLK_DEV // PIECES
     remote = functools.partial(pltpu.make_async_remote_copy, device_id_type=MESH)
 
-    barrier = pltpu.get_barrier_semaphore()
-    for k in range(1, count):
-        pl.semaphore_signal(barrier, inc=1, device_id=((v + k) % count, t), device_id_type=MESH)
-    pl.semaphore_signal(barrier, inc=1, device_id=(v, beside), device_id_type=MESH)
     pairs = (
         (vis_hbm, vis),
         (u_cell_hbm, u_cell),
@@ -333,7 +335,13 @@
     )
     loads = [pltpu.make_async_copy(src, dst, in_sem.at[i]) for i, (src, dst) in enumerate(pairs)]
     loads = [loads[6]] + loads[:6] + loads[7:]
-    for load in loads:
+    for load in loads[:7]:
+        load.start()
+    barrier = pltpu.get_barrier_semaphore()
+    for k in range(1, count):
+        pl.semaphore_signal(barrier, inc=1, device_id=((v + k) % count, t), device_id_type=MESH)
+    pl.semaphore_signal(barrier, inc=1, device_id=(v, beside), device_id_type=MESH)
+    for load in loads[7:]:
         load.start()
     table[...] = jnp.zeros_like(table)
 
@@ -342,18 +350,7 @@
     for load in loads[1:]:
         load.wait()
     stack_features(vis, (u_cell, v_cell, u_frac, v_frac, w_plane), feat)
-    rest = jnp.zeros((1, LANES - 3 * BLK_DEV), jnp.int32)
-    facts = [tiles[...], anchors[pl.ds(0, 1), :], anchors[pl.ds(1, 1), :], rest]
-    meta[...] = jnp.concatenate(facts, axis=1)
     table[pl.ds(0, TAPS), :] = taps[...].astype(jnp.bfloat16).astype(jnp.float32)
-    cells = lax.broadcasted_iota(jnp.int32, (SUB, SUB * POLC), 0)
-    repeat = cells == lax.broadcasted_iota(jnp.int32, (SUB, SUB * POLC), 1) // POLC
-    taper[...] = jnp.dot(
-        gain[...],
-        jnp.where(repeat, 1.0, 0.0),
-        precision=lax.Precision.HIGHEST,
-        preferred_element_type=jnp.float32,
-    )
     pl.semaphore_wait(barrier, count)
 
     def piece(i):
@@ -429,9 +426,6 @@
             device_id=(v, beside),
         )
 
-    for k in range(1, count):
-        tell(k).start()
-    meta_out[c, v] = meta[...]
 
     cells = lax.broadcasted_iota(jnp.int32, (chunk, rows), 0).astype(jnp.float32)
     cells = cells.astype(jnp.bfloat16)
@@ -482,6 +476,20 @@
 
     sort(0, 0)
     lax.fori_loop(0, height, two_steps, 0)
+    rest = jnp.zeros((1, LANES - 3 * BLK_DEV), jnp.int32)
+    facts = [tiles[...], anchors[pl.ds(0, 1), :], anchors[pl.ds(1, 1), :], rest]
+    meta[...] = jnp.concatenate(facts, axis=1)
+    for k in range(1, count):
+        tell(k).start()
+    meta_out[c, v] = meta[...]
+    cells = lax.broadcasted_iota(jnp.int32, (SUB, SUB * POLC), 0)
+    repeat = cells == lax.broadcasted_iota(jnp.int32, (SUB, SUB * POLC), 1) // POLC
+    taper[...] = jnp.dot(
+        gain[...],
+        jnp.where(repeat, 1.0, 0.0),
+        precision=lax.Precision.HIGHEST,
+        preferred_element_type=jnp.float32,
+    )
     for i in range(PIECES):
         whole = partial[piece(i)]
         for j in range(1, height):
@@ -539,10 +547,8 @@
     pass_meta().wait_send()
     for k in range(1, count):
         tell(k).wait_send()
-    for parity in range(2):
-        for source in range(count):
-            facts = meta_out[parity, source]
-            meta_out[parity, source] = placement(facts, tile_rows, v, t)
+    facts = meta_out[...].reshape(2 * count, LANES)
+    meta_out[...] = placement(facts, tile_rows, v, t).reshape(2, count, 1, LANES)
     for i in range(PIECES):
         for j in range(height):
             add_x(j, i).wait_send()
@@ -567,6 +573,13 @@
     canvas[:, pl.ds(SUB, height), :] = jnp.zeros((tiles, height, width + LANES), jnp.float32)
 
     def add_source(source, _):
+        @pl.when(meta[source, FLAGS * BLK_DEV + lane] > 0)
+        def _():
+            add_blocks(source)
+
+        return 0
+
+    def add_blocks(source):
         for b in range(BLK_DEV):
             low = meta[source, lane + b]
 
@@ -580,10 +593,10 @@
                 sub = pltpu.roll(sub, low % ROWS, 0)
                 top = pl.multiple_of(low // ROWS * ROWS, ROWS)
                 base = pl.multiple_of(column // LANES * LANES, LANES)
-                here = (meta[source, b], pl.ds(top, SUB + ROWS), pl.ds(base, span + LANES))
+                place = meta[source, b] if tiles > 1 else 0
+                here = (place, pl.ds(top, SUB + ROWS), pl.ds(base, span + LANES))
                 canvas[here] = canvas[here] + sub
 
-        return 0
 
     lax.fori_loop(0, subs.shape[0], add_source, 0)
     out[...] = canvas[:, pl.ds(SUB, height), pl.ds(0, width)].astype(out.dtype)
@@ -843,7 +856,7 @@
         meta = meta.reshape(2 * vis_count, LANES)
         subs = subs.reshape((2 * vis_count, BLK_DEV) + block)
 
-        def canvas(lane, dtype):
+        def canvas(lane, tiles, dtype):
             return pl.pallas_call(
                 functools.partial(canvas_kernel, lane),
                 grid_spec=pltpu.PrefetchScalarGridSpec(
@@ -852,10 +865,10 @@
                     in_specs=[vmem],
                     out_specs=vmem,
                     scratch_shapes=[
-                        pltpu.VMEM((gt_dev, height + 2 * SUB + ROWS, width + LANES), jnp.float32),
+                        pltpu.VMEM((tiles, height + 2 * SUB + ROWS, width + LANES), jnp.float32),
                     ],
                 ),
-                out_shape=jax.ShapeDtypeStruct((gt_dev, height, width), dtype),
+                out_shape=jax.ShapeDtypeStruct((tiles, height, width), dtype),
                 compiler_params=pltpu.CompilerParams(vmem_limit_bytes=VMEM_BYTES),
                 cost_estimate=pl.CostEstimate(
                     flops=GT * TS * width, bytes_accessed=8 * subs.size, transcendentals=0
@@ -864,8 +877,12 @@
             )(meta, subs)
 
         across = [(tile, (tile + 2) % tile_width) for tile in range(tile_width)]
-        other = lax.ppermute(canvas(3 * BLK_DEV, jnp.bfloat16), "tile", across)
-        return canvas(BLK_DEV, jnp.float32) + other.astype(jnp.float32)
+        others = [
+            lax.ppermute(canvas((3 + g) * BLK_DEV, 1, jnp.bfloat16), "tile", across)
+            for g in range(gt_dev)
+        ]
+        own = canvas(BLK_DEV, gt_dev, jnp.float32)
+        return own + jnp.concatenate(others, axis=0).astype(jnp.float32)
 
     send, table, taper = pl.pallas_call(
         functools.partial(dispatch_kernel, slot_cap),

time: 51.5 us -> 50.7 us (0.984)
  waiting for transfers between devices: 4.56 us -> 2.39 us
  starting transfers between devices: 1.79 us -> 2.59 us
  Pallas kernels: 44.1 us -> 44.7 us
    ppermute x1 -> x2, waiting for transfers between devices: 4.56 us -> 2.39 us  [on_device(): lax.ppermute(canvas((3 + g) * BLK_DEV, 1, jnp.bfloat16), 'tile', across)]
    ppermute x1 -> x2, starting transfers between devices: 1.79 us -> 2.59 us  [on_device(): lax.ppermute(canvas((3 + g) * BLK_DEV, 1, jnp.bfloat16), 'tile', across)]
    pallas_call x2 -> x3, Pallas kernels: 4.64 us -> 4.85 us  [canvas(): pl.pallas_call(functools.partial(canvas_kernel, lane), grid_spec=pltpu.Pr...]
  transfers between devices with their start and end apart: 1 -> 2, of which waited for: 1 -> 1; matrix products, arithmetic and copies ran while one was open for 0% -> 0% of each run, Pallas kernels for 5% -> 6%
where the time goes in v6:
time: 50.7 us; the launch traced here: 50.6 us
  Pallas kernels  44.7 us (88%)
  starting transfers between devices  2.59 us (5%)
  waiting for transfers between devices  2.39 us (5%)
  other arithmetic  0.84 us (2%)
    pallas_call x1, Pallas kernels, on_device(): pl.pallas_call(functools.partial(reduce_kernel, slot_cap, height), in_spe...  39.9 us
    pallas_call x3, Pallas kernels, canvas(): pl.pallas_call(functools.partial(canvas_kernel, lane), grid_spec=pltpu.Pr...  4.85 us
    ppermute x2, starting transfers between devices, on_device(): lax.ppermute(canvas((3 + g) * BLK_DEV, 1, jnp.bfloat16), 'tile', across)  2.59 us
    ppermute x2, waiting for transfers between devices, on_device(): lax.ppermute(canvas((3 + g) * BLK_DEV, 1, jnp.bfloat16), 'tile', across)  2.39 us
  transfers between devices with their start and end apart: 2, of which 1 were waited for; matrix products, arithmetic and copies ran while one was open for 0% of the time, Pallas kernels for 6%

profile of v6, /device:TPU:0, one launch (start us, length us, event | category | flops | bytes accessed | tf_op | source)
XLA Modules:
  0.0 50.6 jit_solution(2472037563562689994)
XLA Ops:
  0.0 39.9 %reduce.1 = (bf16[2,8,8,32,256]{4,3,2,1,0:T(8,128)(2,1)S(1)}, s32[2,8,1,128]{3,2,1,0:T(1,128)S(1)}) custom-call(bf16[1024,128]{1,0:T(8,128)(2,1)} %vis_hbm.1, s32[16,1024]{1,0:T(8,128)} %u_cell_hbm.1, s32[16,1024]{1,0:T(8,128)} %v_cell_hbm.1, s32[16,1024]{1,0:T(8,128)} %u_frac_hbm.1, s32[16,1024]{1,0:T(8,128)} %v_frac_hbm.1, s32[16,1024]{1,0:T(8,128)} %w_plane_hbm.1, ...), custom_call_target="tpu_custom_call" | custom-call | tf_op jit(solution)/shard_map/reduce/pallas_call | solution.py:815
  39.9 1.8 %canvas.4 = bf16[1,32,2048]{2,1,0:T(8,128)(2,1)S(1)} custom-call(s32[16,128]{1,0:T(8,128)S(1)} %bitcast.9, bf16[16,8,32,256]{3,2,1,0:T(8,128)(2,1)S(1)} %bitcast.6), custom_call_target="tpu_custom_call" | custom-call | flops 4194304 | bytes 8388608 | tf_op jit(solution)/shard_map/canvas/pallas_call | solution.py:860
  41.7 1.1 %collective-permute-start = (bf16[1,32,2048]{2,1,0:T(8,128)(2,1)S(1)}, bf16[1,32,2048]{2,1,0:T(8,128)(2,1)S(1)}, u32[]{:S(2)}, u32[]{:S(2)}) collective-permute-start(bf16[1,32,2048]{2,1,0:T(8,128)(2,1)S(1)} %canvas.4), channel_id=1, source_target_pairs={{0,2},{1,3},{2,0},{3,1},{4,6},{5,7},{6,4},{7,5},{8,10},{9,11},{10,... | collective-permute-start | bytes 393224 | tf_op jit(solution)/shard_map/ppermute | solution.py:881
  42.8 1.3 %canvas.5 = bf16[1,32,2048]{2,1,0:T(8,128)(2,1)S(1)} custom-call(s32[16,128]{1,0:T(8,128)S(1)} %bitcast.10, bf16[16,8,32,256]{3,2,1,0:T(8,128)(2,1)S(1)} %bitcast.7), custom_call_target="tpu_custom_call" | custom-call | flops 4194304 | bytes 8388608 | tf_op jit(solution)/shard_map/canvas/pallas_call | solution.py:860
  44.0 1.5 %collective-permute-start.1 = (bf16[1,32,2048]{2,1,0:T(8,128)(2,1)S(1)}, bf16[1,32,2048]{2,1,0:T(8,128)(2,1)S(1)}, u32[]{:S(2)}, u32[]{:S(2)}) collective-permute-start(bf16[1,32,2048]{2,1,0:T(8,128)(2,1)S(1)} %canvas.5), channel_id=1, source_target_pairs={{0,2},{1,3},{2,0},{3,1},{4,6},{5,7},{6,4},{7,5},{8,10},{9,11},{10,... | collective-permute-start | bytes 393224 | tf_op jit(solution)/shard_map/ppermute | solution.py:881
  45.5 1.8 %canvas.3 = f32[2,32,2048]{2,1,0:T(8,128)S(1)} custom-call(s32[16,128]{1,0:T(8,128)S(1)} %bitcast.11, bf16[16,8,32,256]{3,2,1,0:T(8,128)(2,1)S(1)} %bitcast.8), custom_call_target="tpu_custom_call" | custom-call | flops 4194304 | bytes 8388608 | tf_op jit(solution)/shard_map/canvas/pallas_call | solution.py:860
  47.4 0.0 collective-permute-done
  47.4 2.4 %collective-permute-done.1 = bf16[1,32,2048]{2,1,0:T(8,128)(2,1)S(1)} collective-permute-done((bf16[1,32,2048]{2,1,0:T(8,128)(2,1)S(1)}, bf16[1,32,2048]{2,1,0:T(8,128)(2,1)S(1)}, u32[]{:S(2)}, u32[]{:S(2)}) %collective-permute-start.1) | collective-permute-done | bytes 131104 | tf_op jit(solution)/shard_map/ppermute | solution.py:881
  49.8 0.8 %convert_add_fusion = f32[2,32,2048]{2,1,0:T(8,128)} fusion(f32[2,32,2048]{2,1,0:T(8,128)S(1)} %canvas.3, bf16[1,32,2048]{2,1,0:T(8,128)(2,1)S(1)} %collective-permute-done.1, bf16[1,32,2048]{2,1,0:T(8,128)(2,1)S(1)} %collective-permute-done), kind=kLoop, calls=%fused_computation | loop fusion | flops 393216 | bytes 1310720 | tf_op jit(solution)/shard_map/add | solution.py:885
Async XLA Ops:
  41.7 5.7 %collective-permute-start = (bf16[1,32,2048]{2,1,0:T(8,128)(2,1)S(1)}, bf16[1,32,2048]{2,1,0:T(8,128)(2,1)S(1)}, u32[]{:S(2)}, u32[]{:S(2)}) collective-permute-start(bf16[1,32,2048]{2,1,0:T(8,128)(2,1)S(1)} %canvas.4), channel_id=1, source_target_pairs={{0,2},{1,3},{2,0},{3,1},{4,6},{5,7},{6,4},{7,5},{8,10},{9,11},{10,... | collective-permute-start | bytes 393224 | tf_op jit(solution)/shard_map/ppermute | solution.py:881
  44.0 5.7 %collective-permute-start.1 = (bf16[1,32,2048]{2,1,0:T(8,128)(2,1)S(1)}, bf16[1,32,2048]{2,1,0:T(8,128)(2,1)S(1)}, u32[]{:S(2)}, u32[]{:S(2)}) collective-permute-start(bf16[1,32,2048]{2,1,0:T(8,128)(2,1)S(1)} %canvas.5), channel_id=1, source_target_pairs={{0,2},{1,3},{2,0},{3,1},{4,6},{5,7},{6,4},{7,5},{8,10},{9,11},{10,... | collective-permute-start | bytes 393224 | tf_op jit(solution)/shard_map/ppermute | solution.py:881

commit v7 on v6

--- a/solution.py
+++ b/solution.py
@@ -598,7 +598,7 @@
                 canvas[here] = canvas[here] + sub
 
 
-    lax.fori_loop(0, subs.shape[0], add_source, 0)
+    lax.fori_loop(0, subs.shape[0], add_source, 0, unroll=2)
     out[...] = canvas[:, pl.ds(SUB, height), pl.ds(0, width)].astype(out.dtype)
 
 

time: 50.7 us -> 51.1 us (level)
  waiting for transfers between devices: 2.39 us -> 4.63 us
  Pallas kernels: 44.7 us -> 43.3 us
  starting transfers between devices: 2.59 us -> 1.99 us
    ppermute x2, waiting for transfers between devices: 2.39 us -> 4.63 us  [on_device(): lax.ppermute(canvas((3 + g) * BLK_DEV, 1, jnp.bfloat16), 'tile', across)]
    pallas_call x3, Pallas kernels: 4.85 us -> 3.38 us  [canvas(): pl.pallas_call(functools.partial(canvas_kernel, lane), grid_spec=pltpu.Pr...]
    ppermute x2, starting transfers between devices: 2.59 us -> 1.99 us  [on_device(): lax.ppermute(canvas((3 + g) * BLK_DEV, 1, jnp.bfloat16), 'tile', across)]
  transfers between devices with their start and end apart: 2 -> 2, of which waited for: 1 -> 2; matrix products, arithmetic and copies ran while one was open for 0% -> 0% of each run, Pallas kernels for 6% -> 5%
where the time goes in v7:
time: 51.1 us; the launch traced here: 50.8 us
  Pallas kernels  43.3 us (85%)
  waiting for transfers between devices  4.63 us (9%)
  starting transfers between devices  1.99 us (4%)
  other arithmetic  0.84 us (2%)
    pallas_call x1, Pallas kernels, on_device(): pl.pallas_call(functools.partial(reduce_kernel, slot_cap, height), in_spe...  39.9 us
    ppermute x2, waiting for transfers between devices, on_device(): lax.ppermute(canvas((3 + g) * BLK_DEV, 1, jnp.bfloat16), 'tile', across)  4.63 us
    pallas_call x3, Pallas kernels, canvas(): pl.pallas_call(functools.partial(canvas_kernel, lane), grid_spec=pltpu.Pr...  3.38 us
    ppermute x2, starting transfers between devices, on_device(): lax.ppermute(canvas((3 + g) * BLK_DEV, 1, jnp.bfloat16), 'tile', across)  1.99 us
  transfers between devices with their start and end apart: 2, of which 2 were waited for; matrix products, arithmetic and copies ran while one was open for 0% of the time, Pallas kernels for 5%

profile of v7, /device:TPU:0, one launch (start us, length us, event | category | flops | bytes accessed | tf_op | source)
XLA Modules:
  0.0 50.8 jit_solution(14356363393054870936)
XLA Ops:
  0.0 39.9 %reduce.1 = (bf16[2,8,8,32,256]{4,3,2,1,0:T(8,128)(2,1)S(1)}, s32[2,8,1,128]{3,2,1,0:T(1,128)S(1)}) custom-call(bf16[1024,128]{1,0:T(8,128)(2,1)} %vis_hbm.1, s32[16,1024]{1,0:T(8,128)} %u_cell_hbm.1, s32[16,1024]{1,0:T(8,128)} %v_cell_hbm.1, s32[16,1024]{1,0:T(8,128)} %u_frac_hbm.1, s32[16,1024]{1,0:T(8,128)} %v_frac_hbm.1, s32[16,1024]{1,0:T(8,128)} %w_plane_hbm.1, ...), custom_call_target="tpu_custom_call" | custom-call | tf_op jit(solution)/shard_map/reduce/pallas_call | solution.py:815
  39.9 1.1 %canvas.4 = bf16[1,32,2048]{2,1,0:T(8,128)(2,1)S(1)} custom-call(s32[16,128]{1,0:T(8,128)S(1)} %bitcast.9, bf16[16,8,32,256]{3,2,1,0:T(8,128)(2,1)S(1)} %bitcast.6), custom_call_target="tpu_custom_call" | custom-call | flops 4194304 | bytes 8388608 | tf_op jit(solution)/shard_map/canvas/pallas_call | solution.py:860
  41.0 1.9 %collective-permute-start = (bf16[1,32,2048]{2,1,0:T(8,128)(2,1)S(1)}, bf16[1,32,2048]{2,1,0:T(8,128)(2,1)S(1)}, u32[]{:S(2)}, u32[]{:S(2)}) collective-permute-start(bf16[1,32,2048]{2,1,0:T(8,128)(2,1)S(1)} %canvas.4), channel_id=1, source_target_pairs={{0,2},{1,3},{2,0},{3,1},{4,6},{5,7},{6,4},{7,5},{8,10},{9,11},{10,... | collective-permute-start | bytes 393224 | tf_op jit(solution)/shard_map/ppermute | solution.py:881
  42.9 1.1 %canvas.5 = bf16[1,32,2048]{2,1,0:T(8,128)(2,1)S(1)} custom-call(s32[16,128]{1,0:T(8,128)S(1)} %bitcast.10, bf16[16,8,32,256]{3,2,1,0:T(8,128)(2,1)S(1)} %bitcast.7), custom_call_target="tpu_custom_call" | custom-call | flops 4194304 | bytes 8388608 | tf_op jit(solution)/shard_map/canvas/pallas_call | solution.py:860
  44.0 0.1 collective-permute-start.1
  44.0 1.3 %canvas.3 = f32[2,32,2048]{2,1,0:T(8,128)S(1)} custom-call(s32[16,128]{1,0:T(8,128)S(1)} %bitcast.11, bf16[16,8,32,256]{3,2,1,0:T(8,128)(2,1)S(1)} %bitcast.8), custom_call_target="tpu_custom_call" | custom-call | flops 4194304 | bytes 8388608 | tf_op jit(solution)/shard_map/canvas/pallas_call | solution.py:860
  45.3 2.1 %collective-permute-done = bf16[1,32,2048]{2,1,0:T(8,128)(2,1)S(1)} collective-permute-done((bf16[1,32,2048]{2,1,0:T(8,128)(2,1)S(1)}, bf16[1,32,2048]{2,1,0:T(8,128)(2,1)S(1)}, u32[]{:S(2)}, u32[]{:S(2)}) %collective-permute-start) | collective-permute-done | bytes 131104 | tf_op jit(solution)/shard_map/ppermute | solution.py:881
  47.4 2.5 %collective-permute-done.1 = bf16[1,32,2048]{2,1,0:T(8,128)(2,1)S(1)} collective-permute-done((bf16[1,32,2048]{2,1,0:T(8,128)(2,1)S(1)}, bf16[1,32,2048]{2,1,0:T(8,128)(2,1)S(1)}, u32[]{:S(2)}, u32[]{:S(2)}) %collective-permute-start.1) | collective-permute-done | bytes 131104 | tf_op jit(solution)/shard_map/ppermute | solution.py:881
  49.9 0.8 %convert_add_fusion = f32[2,32,2048]{2,1,0:T(8,128)} fusion(f32[2,32,2048]{2,1,0:T(8,128)S(1)} %canvas.3, bf16[1,32,2048]{2,1,0:T(8,128)(2,1)S(1)} %collective-permute-done.1, bf16[1,32,2048]{2,1,0:T(8,128)(2,1)S(1)} %collective-permute-done), kind=kLoop, calls=%fused_computation | loop fusion | flops 393216 | bytes 1310720 | tf_op jit(solution)/shard_map/add | solution.py:885
Async XLA Ops:
  41.0 6.4 %collective-permute-start = (bf16[1,32,2048]{2,1,0:T(8,128)(2,1)S(1)}, bf16[1,32,2048]{2,1,0:T(8,128)(2,1)S(1)}, u32[]{:S(2)}, u32[]{:S(2)}) collective-permute-start(bf16[1,32,2048]{2,1,0:T(8,128)(2,1)S(1)} %canvas.4), channel_id=1, source_target_pairs={{0,2},{1,3},{2,0},{3,1},{4,6},{5,7},{6,4},{7,5},{8,10},{9,11},{10,... | collective-permute-start | bytes 393224 | tf_op jit(solution)/shard_map/ppermute | solution.py:881
  44.0 6.0 %collective-permute-start.1 = (bf16[1,32,2048]{2,1,0:T(8,128)(2,1)S(1)}, bf16[1,32,2048]{2,1,0:T(8,128)(2,1)S(1)}, u32[]{:S(2)}, u32[]{:S(2)}) collective-permute-start(bf16[1,32,2048]{2,1,0:T(8,128)(2,1)S(1)} %canvas.5), channel_id=1, source_target_pairs={{0,2},{1,3},{2,0},{3,1},{4,6},{5,7},{6,4},{7,5},{8,10},{9,11},{10,... | collective-permute-start | bytes 393224 | tf_op jit(solution)/shard_map/ppermute | solution.py:881
